TPU v7x, 256 devices: a whole 4x4x8 slice. The times are simulated.
256 devices in a mesh: pipe: 4 (over y_hi, core), expert: 64 (over y_lo, z, x).
Axes of the slice: x: 4, y: 4 (y_hi: 2, y_lo: 2; y = y_hi * 2 + y_lo), z: 8, core: 2. Of those that a mesh axis runs over, the one named last changes fastest.
Arguments:
- tokens: bfloat16 [8192, 7168], P('expert', 'pipe'), may hold values from -6 to 6
- grad_out: bfloat16 [8192, 7168], P('expert', 'pipe'), may hold values from -6 to 6
- routed_expert_index: int32 [8192, 8], P('expert'), may hold values from 0 to 255, as said below
- route_gates: bfloat16 [8192, 8], P('expert'), may hold values from 0.099609375 to 0.5
- gate_up: bfloat16 [2, 7168, 8192], P(None, 'pipe', 'expert'), may hold values from -0.0625 to 0.0625
- gate_up_m: bfloat16 [2, 7168, 8192], P(None, 'pipe', 'expert'), may hold values from -24 to 24
- gate_up_v: bfloat16 [2, 7168, 8192], P(None, 'pipe', 'expert'), may hold values from 4 to 400
- down: bfloat16 [8192, 7168], P('expert', 'pipe'), may hold values from -0.1875 to 0.1875
- down_m: bfloat16 [8192, 7168], P('expert', 'pipe'), may hold values from -12 to 12
- down_v: bfloat16 [8192, 7168], P('expert', 'pipe'), may hold values from 1 to 100
Outputs:
- mixed: bfloat16 [8192, 7168], P('expert', 'pipe')
- grad_tokens: bfloat16 [8192, 7168], P('expert', 'pipe')
- gate_up_new: bfloat16 [2, 7168, 8192], P(None, 'pipe', 'expert')
- gate_up_m_new: bfloat16 [2, 7168, 8192], P(None, 'pipe', 'expert')
- gate_up_v_new: bfloat16 [2, 7168, 8192], P(None, 'pipe', 'expert')
- down_new: bfloat16 [8192, 7168], P('expert', 'pipe')
- down_m_new: bfloat16 [8192, 7168], P('expert', 'pipe')
- down_v_new: bfloat16 [8192, 7168], P('expert', 'pipe')
Inputs may be any that keep to these rules, and one draw needn't show every extreme that they name: `routed_expert_index`: each token names 8 different experts. In each aligned block of 128 tokens, every expert below 8 is named by 1 to 16 of the tokens, and one of them by exactly 16.
All inputs are finite; a program needn't handle non-finite values.
Results may differ from a plain program's by a relative error of at most 0.0058.
Values may be sent and summed in bfloat16 or wider, within the bound.
No kernel may reach another device: no remote copies, remote signals or barrier semaphores. Data moves between devices by JAX's collectives and lax.ppermute only.
A program may use at most 128 MiB of HBM per device.

v0:
```python
import jax
import jax.numpy as jnp
from jax import lax
from jax.sharding import PartitionSpec as P

GROUP = 8


beta_first = 0.9
beta_second = 0.95
learning_rate = 0.00022
decay_rate = 0.1
epsilon = 1e-08


def adamw(weight, moment_one, moment_two, gradient):
    weight_real = weight.astype(jnp.float32)
    first_new = beta_first * moment_one.astype(jnp.float32) + (1.0 - beta_first) * gradient
    second_new = (
        beta_second * moment_two.astype(jnp.float32) + (1.0 - beta_second) * gradient * gradient
    )
    weight_new = weight_real - learning_rate * (
        first_new / (jnp.sqrt(second_new) + epsilon) + decay_rate * weight_real
    )
    return (
        weight_new.astype(jnp.bfloat16),
        first_new.astype(jnp.bfloat16),
        second_new.astype(jnp.bfloat16),
    )


def per_device(
    tokens,
    grad_out,
    routed_expert_index,
    route_gates,
    gate_up,
    gate_up_m,
    gate_up_v,
    down,
    down_m,
    down_v,
):
    devices = lax.axis_size("expert")
    expert_list = devices // GROUP
    tok_dev, width_dev = tokens.shape
    expert_capacity = GROUP * tok_dev // devices
    hidden = gate_up.shape[2]
    total_rows = devices * expert_capacity
    onehot = (routed_expert_index[:, :, None] == jnp.arange(expert_list, dtype=jnp.int32)).astype(
        jnp.int32
    )
    per_token = jnp.sum(onehot, axis=1)
    before = jnp.cumsum(per_token, axis=0) - per_token
    slot_index = jnp.sum(onehot * before[:, None, :], axis=2)
    active_experts = routed_expert_index < expert_list
    placing = (slot_index[:, :, None] == jnp.arange(expert_capacity, dtype=jnp.int32)).astype(
        jnp.float32
    )
    onehot_real = onehot.astype(jnp.float32)
    selector = jnp.einsum("tke,tkc->ect", onehot_real, placing).astype(jnp.bfloat16)
    slot_gates = jnp.einsum(
        "tke,tkc,tk->ec", onehot_real, placing, route_gates.astype(jnp.float32)
    ).astype(jnp.bfloat16)
    flattened_index = jnp.where(
        active_experts, routed_expert_index * expert_capacity + slot_index, 0
    )
    routing_weight = active_experts.astype(jnp.float32)

    def fan_out(buffer):
        spread = jnp.broadcast_to(buffer[:, None], (expert_list, GROUP) + buffer.shape[1:])
        return spread.reshape((devices,) + buffer.shape[1:])

    def place_rows(source):
        placed = jnp.einsum("ect,td->ecd", selector, source, preferred_element_type=jnp.float32)
        return fan_out(placed.astype(jnp.bfloat16))

    def gather_routes(received):
        row_table = jnp.sum(
            received.reshape(expert_list, GROUP, expert_capacity, width_dev).astype(jnp.float32),
            axis=1,
        )
        row_table = row_table.reshape(expert_list * expert_capacity, width_dev)
        picked = jnp.take(row_table, flattened_index, axis=0)
        return jnp.sum(picked * routing_weight[:, :, None], axis=1).astype(jnp.bfloat16)

    rows_in, gates_in = (
        lax.all_to_all(place_rows(tokens), "expert", split_axis=0, concat_axis=0, tiled=True),
        lax.all_to_all(fan_out(slot_gates), "expert", split_axis=0, concat_axis=0, tiled=True),
    )
    row_data = rows_in.reshape(total_rows, width_dev)
    row_gates = gates_in.reshape(total_rows)
    paired = jnp.concatenate((gate_up[0], gate_up[1]), axis=1)

    def forward_rows(row_piece, gate_piece):
        pre_sums = jnp.dot(row_piece, paired, preferred_element_type=jnp.float32)
        pre_sums = lax.psum(pre_sums, "pipe")
        gate_pre = pre_sums[:, :hidden]
        up_pre = pre_sums[:, hidden:]
        scaled = (gate_piece.astype(jnp.float32)[:, None] * jax.nn.silu(gate_pre) * up_pre).astype(
            jnp.bfloat16
        )
        partial_rows = jnp.dot(scaled, down, preferred_element_type=jnp.float32).astype(
            jnp.bfloat16
        )
        return ((partial_rows, scaled, gate_pre, up_pre), ())

    def backward_rows(row_piece, gate_piece, gate_pre, up_pre, scaled, grad_piece):
        back_prop = lax.dot_general(
            grad_piece, down, (((1,), (1,)), ((), ())), preferred_element_type=jnp.float32
        )
        back_prop = lax.psum(back_prop, "pipe")
        d_hidden = gate_piece.astype(jnp.float32)[:, None] * back_prop
        sigmoid_gate = jax.nn.sigmoid(gate_pre)
        d_gate = d_hidden * up_pre * sigmoid_gate * (1.0 + gate_pre * (1.0 - sigmoid_gate))
        d_up = d_hidden * gate_pre * sigmoid_gate
        d_paired = jnp.concatenate((d_gate.astype(jnp.bfloat16), d_up.astype(jnp.bfloat16)), axis=1)
        delta_rows = lax.dot_general(
            d_paired, paired, (((1,), (1,)), ((), ())), preferred_element_type=jnp.float32
        ).astype(jnp.bfloat16)
        grad_paired = lax.dot_general(
            row_piece, d_paired, (((0,), (0,)), ((), ())), preferred_element_type=jnp.float32
        )
        grad_down = lax.dot_general(
            scaled, grad_piece, (((0,), (0,)), ((), ())), preferred_element_type=jnp.float32
        )
        return ((delta_rows,), (grad_paired, grad_down))

    def apply_rows(row_fn, inputs):
        return row_fn(*inputs)

    (partial_rows, scaled, gate_pre, up_pre), unused = apply_rows(
        forward_rows, (row_data, row_gates)
    )
    partial_send = partial_rows.reshape(devices, expert_capacity, width_dev)
    grad_send = place_rows(grad_out)
    returned = lax.all_to_all(partial_send, "expert", split_axis=0, concat_axis=0, tiled=True)
    grad_in = lax.all_to_all(grad_send, "expert", split_axis=0, concat_axis=0, tiled=True)
    mixed = gather_routes(returned)
    grad_rows = grad_in.reshape(total_rows, width_dev)
    (delta_rows,), (grad_paired, grad_down) = apply_rows(
        backward_rows, (row_data, row_gates, gate_pre, up_pre, scaled, grad_rows)
    )
    delta_send = delta_rows.reshape(devices, expert_capacity, width_dev)
    returned_delta = lax.all_to_all(delta_send, "expert", split_axis=0, concat_axis=0, tiled=True)
    grad_tokens = gather_routes(returned_delta)
    grad_stack = jnp.stack((grad_paired[:, :hidden], grad_paired[:, hidden:]), axis=0)
    gate_up_new, gate_up_m_new, gate_up_v_new = adamw(gate_up, gate_up_m, gate_up_v, grad_stack)
    down_new, down_m_new, down_v_new = adamw(down, down_m, down_v, grad_down)
    return (
        mixed,
        grad_tokens,
        gate_up_new,
        gate_up_m_new,
        gate_up_v_new,
        down_new,
        down_m_new,
        down_v_new,
    )


def solution(mesh):
    placed = (
        P("expert", "pipe"),
        P("expert", "pipe"),
        P("expert", None),
        P("expert", None),
        P(None, "pipe", "expert"),
        P(None, "pipe", "expert"),
        P(None, "pipe", "expert"),
        P("expert", "pipe"),
        P("expert", "pipe"),
        P("expert", "pipe"),
    )
    return jax.shard_map(
        per_device,
        mesh=mesh,
        in_specs=placed,
        out_specs=(
            P("expert", "pipe"),
            P("expert", "pipe"),
            P(None, "pipe", "expert"),
            P(None, "pipe", "expert"),
            P(None, "pipe", "expert"),
            P("expert", "pipe"),
            P("expert", "pipe"),
            P("expert", "pipe"),
        ),
        check_vma=False,
    )
```

profile of v0, /device:TPU:6, one launch (start us, length us, event | category | flops | bytes accessed | tf_op | source)
XLA Modules:
  0.0 478.9 jit_solution(5532890862571923946)
XLA Ops:
  7.2 0.8 copy.63
  8.0 2.2 convert_reduce_fusion.2
  10.7 0.3 fusion.8
  11.5 2.1 broadcast_in_dim.19
  13.6 13.3 %all-to-all-start.3 = ((bf16[64,16,1792]{2,1,0:T(8,128)(2,1)}), bf16[64,16,1792]{2,1,0:T(8,128)(2,1)}, u32[]{:S(2)}, u32[]{:S(2)}) async-start(bf16[64,16,1792]{2,1,0:T(8,128)(2,1)} %bitcast.64), calls=%async_computation.3 | async-start | bytes 7340032 | tf_op jit(solution)/shard_map/all_to_all | solution.py:138
  26.9 0.3 convolution_convert_fusion.3
  27.2 84.7 %all-to-all-done.3 = bf16[64,16,1792]{2,1,0:T(8,128)(2,1)} async-done(((bf16[64,16,1792]{2,1,0:T(8,128)(2,1)}), bf16[64,16,1792]{2,1,0:T(8,128)(2,1)}, u32[]{:S(2)}, u32[]{:S(2)}) %all-to-all-start.3) | async-done | bytes 3670048 | tf_op jit(solution)/shard_map/all_to_all | solution.py:138
  111.9 2.2 broadcast_in_dim.17
  114.1 5.7 %all-to-all-start.1 = ((bf16[64,16,1792]{2,1,0:T(8,128)(2,1)}), bf16[64,16,1792]{2,1,0:T(8,128)(2,1)}, u32[]{:S(2)}, u32[]{:S(2)}) async-start(bf16[64,16,1792]{2,1,0:T(8,128)(2,1)} %bitcast.62), calls=%async_computation.1 | async-start | bytes 7340032 | tf_op jit(solution)/shard_map/all_to_all | solution.py:88
  120.0 3.9 fusion.29
  123.9 80.8 %all-to-all-done.1 = bf16[64,16,1792]{2,1,0:T(8,128)(2,1)} async-done(((bf16[64,16,1792]{2,1,0:T(8,128)(2,1)}), bf16[64,16,1792]{2,1,0:T(8,128)(2,1)}, u32[]{:S(2)}, u32[]{:S(2)}) %all-to-all-start.1) | async-done | bytes 3670048 | tf_op jit(solution)/shard_map/all_to_all | solution.py:88
  204.7 4.2 fusion.16
  209.3 0.3 fusion.19
  209.8 14.3 %all_to_all.29 = bf16[64,1,16]{2,1,0:T(2,128)(2,1)S(1)} all-to-all(bf16[64,1,16]{2,1,0:T(2,128)(2,1)S(1)} %copy.69), channel_id=1, replica_groups=mesh['pipe'=4,'expert'=64] {'expert'}, dimensions={0} | all-to-all | bytes 4096 | tf_op jit(solution)/shard_map/all_to_all | solution.py:89
  224.3 37.2 %all-reduce.3.cloned.1.call-done = (f32[1024,128]{1,0:T(8,128)}, f32[1024,256]{1,0:T(8,128)}) async-done(((f32[1024,128]{1,0:T(8,128)}, f32[1024,256]{1,0:T(8,128)}), (f32[1024,128]{1,0:T(8,128)}, f32[1024,256]{1,0:T(8,128)})) %all-reduce.3.cloned.1.call-update) | async-done | bytes 1572880 | tf_op jit(solution)/shard_map/psum | solution.py:112
  261.5 1.7 multiply_convert_fusion.1
  263.2 2.9 convolution_convert_fusion
  266.1 10.7 %all-to-all-start.2 = ((bf16[64,16,1792]{2,1,0:T(8,128)(2,1)}), bf16[64,16,1792]{2,1,0:T(8,128)(2,1)}, u32[]{:S(2)}, u32[]{:S(2)}) async-start(bf16[64,16,1792]{2,1,0:T(8,128)(2,1)} %bitcast.63), calls=%async_computation.2 | async-start | bytes 7340032 | tf_op jit(solution)/shard_map/all_to_all | solution.py:137
  276.9 3.1 convolution_convert_fusion.1
  279.9 82.4 %all-to-all-done.2 = bf16[64,16,1792]{2,1,0:T(8,128)(2,1)} async-done(((bf16[64,16,1792]{2,1,0:T(8,128)(2,1)}), bf16[64,16,1792]{2,1,0:T(8,128)(2,1)}, u32[]{:S(2)}, u32[]{:S(2)}) %all-to-all-start.2) | async-done | bytes 3670048 | tf_op jit(solution)/shard_map/all_to_all | solution.py:137
  362.3 5.7 %all-to-all-start.4 = ((bf16[64,16,1792]{2,1,0:T(8,128)(2,1)}), bf16[64,16,1792]{2,1,0:T(8,128)(2,1)}, u32[]{:S(2)}, u32[]{:S(2)}) async-start(bf16[64,16,1792]{2,1,0:T(8,128)(2,1)} %bitcast.61), calls=%async_computation.4 | async-start | bytes 7340032 | tf_op jit(solution)/shard_map/all_to_all | solution.py:145
  368.6 3.3 fusion.23
  371.9 4.4 fusion.20
  376.4 1.1 copy-done.3
  377.5 0.3 copy-done.4
  377.8 3.1 fusion.15
  380.8 2.6 convert_reduce_fusion.1
  383.5 6.7 %gather_fusion = f32[1024,1792]{1,0:T(8,128)} fusion(f32[128,1792]{1,0:T(8,128)S(1)} %bitcast.60, s32[1024]{0:T(1024)S(1)} %broadcast_clamp_fusion), kind=kCustom, calls=%fused_computation.clone | custom fusion | bytes 14684160 | tf_op jit(solution)/shard_map/jit(_take)/gather | solution.py:84
  390.2 62.7 %all-to-all-done.4 = bf16[64,16,1792]{2,1,0:T(8,128)(2,1)} async-done(((bf16[64,16,1792]{2,1,0:T(8,128)(2,1)}), bf16[64,16,1792]{2,1,0:T(8,128)(2,1)}, u32[]{:S(2)}, u32[]{:S(2)}) %all-to-all-start.4) | async-done | bytes 3670048 | tf_op jit(solution)/shard_map/all_to_all | solution.py:145
  452.9 2.6 convert_reduce_fusion
  455.5 6.7 %gather_fusion.1 = f32[1024,1792]{1,0:T(8,128)} fusion(f32[128,1792]{1,0:T(8,128)S(1)} %bitcast.59, s32[1024]{0:T(1024)S(1)} %broadcast_clamp_fusion), kind=kCustom, calls=%fused_computation.1.clone | custom fusion | bytes 14684160 | tf_op jit(solution)/shard_map/jit(_take)/gather | solution.py:84
  462.2 9.8 %fusion.1 = (bf16[128,1792]{1,0:T(8,128)(2,1)}, bf16[128,1792]{1,0:T(8,128)(2,1)}) fusion(f32[1024,1792]{1,0:T(8,128)} %gather_fusion.1, f32[128,8]{1,0:T(8,128)S(1)} %copy.72, pred[128,8]{1,0:T(8,128)(4,1)S(1)} %copy.65, f32[1024,1792]{1,0:T(8,128)} %gather_fusion), kind=kLoop, calls=%fused_computation.6 | loop fusion | flops 10551296 | bytes 15602688 | tf_op jit(solution)/shard_map/reduce_sum | solution.py:85
  (46 shorter events, 2.4 us)
Async XLA Ops:
  7.2 4.1 copy-start
  10.7 198.6 %copy-start.5 = (s32[128,8]{1,0:T(8,128)}, s32[128,8]{1,0:T(8,128)S(1)}, u32[]{:S(2)}) copy-start(s32[128,8]{1,0:T(8,128)S(1)} %select_reduce_fusion) | copy-start | bytes 12292
  13.6 13.3 %copy-start.7 = (bf16[128,1792]{1,0:T(8,128)(2,1)S(1)}, bf16[128,1792]{1,0:T(8,128)(2,1)}, u32[]{:S(2)}) copy-start(bf16[128,1792]{1,0:T(8,128)(2,1)} %param.12) | copy-start | bytes 1376260
  13.6 98.3 %all-to-all-start.3 = ((bf16[64,16,1792]{2,1,0:T(8,128)(2,1)}), bf16[64,16,1792]{2,1,0:T(8,128)(2,1)}, u32[]{:S(2)}, u32[]{:S(2)}) async-start(bf16[64,16,1792]{2,1,0:T(8,128)(2,1)} %bitcast.64), calls=%async_computation.3 | async-start | bytes 7340032 | tf_op jit(solution)/shard_map/all_to_all | solution.py:138
  114.1 5.8 %copy-start.1 = (bf16[2,1792,128]{2,1,0:T(8,128)(2,1)S(1)}, bf16[2,1792,128]{2,1,0:T(8,128)(2,1)}, u32[]{:S(2)}) copy-start(bf16[2,1792,128]{2,1,0:T(8,128)(2,1)} %param.16) | copy-start | bytes 2752516
  114.1 5.8 %copy-start.2 = (bf16[128,1792]{1,0:T(8,128)(2,1)S(1)}, bf16[128,1792]{1,0:T(8,128)(2,1)}, u32[]{:S(2)}) copy-start(bf16[128,1792]{1,0:T(8,128)(2,1)} %param.19) | copy-start | bytes 1376260
  114.1 90.6 %all-to-all-start.1 = ((bf16[64,16,1792]{2,1,0:T(8,128)(2,1)}), bf16[64,16,1792]{2,1,0:T(8,128)(2,1)}, u32[]{:S(2)}, u32[]{:S(2)}) async-start(bf16[64,16,1792]{2,1,0:T(8,128)(2,1)} %bitcast.62), calls=%async_computation.1 | async-start | bytes 7340032 | tf_op jit(solution)/shard_map/all_to_all | solution.py:88
  119.8 141.7 %all-reduce.3.cloned.1.call-start = ((), (), s32[]{:S(2)}) async-start(), calls=%async_computation.5 | async-start | bytes 3145728 | tf_op jit(solution)/shard_map/psum | solution.py:112
  204.7 4.2 copy-start.9
  266.1 96.2 %all-to-all-start.2 = ((bf16[64,16,1792]{2,1,0:T(8,128)(2,1)}), bf16[64,16,1792]{2,1,0:T(8,128)(2,1)}, u32[]{:S(2)}, u32[]{:S(2)}) async-start(bf16[64,16,1792]{2,1,0:T(8,128)(2,1)} %bitcast.63), calls=%async_computation.2 | async-start | bytes 7340032 | tf_op jit(solution)/shard_map/all_to_all | solution.py:137
  362.3 5.7 %copy-start.6 = (s32[128,8]{1,0:T(8,128)S(1)}, s32[128,8]{1,0:T(8,128)}, u32[]{:S(2)}) copy-start(s32[128,8]{1,0:T(8,128)} %copy-done.5) | copy-start | bytes 12292
  362.3 5.8 %copy-start.8 = (s32[128,8]{0,1:T(8,128)S(1)}, s32[128,8]{0,1:T(8,128)}, u32[]{:S(2)}) copy-start(s32[128,8]{0,1:T(8,128)} %param.14) | copy-start | bytes 12292
  362.3 90.6 %all-to-all-start.4 = ((bf16[64,16,1792]{2,1,0:T(8,128)(2,1)}), bf16[64,16,1792]{2,1,0:T(8,128)(2,1)}, u32[]{:S(2)}, u32[]{:S(2)}) async-start(bf16[64,16,1792]{2,1,0:T(8,128)(2,1)} %bitcast.61), calls=%async_computation.4 | async-start | bytes 7340032 | tf_op jit(solution)/shard_map/all_to_all | solution.py:145
  368.5 3.3 copy-start.10
  368.6 3.3 copy-start.11
  376.3 1.2 copy-start.3
  376.3 1.5 copy-start.4
Sparse Core Ops, SparseCore 0:
  209.0 52.4 all-reduce.2
where the time goes:
time: 480 us; the launch traced here: 479 us
  waiting for transfers between devices  348 us (72%)
  starting transfers between devices  35.5 us (7%)
  other arithmetic  23 us (5%)
  matrix products  22.9 us (5%)
  local copies, waits for them, and re-layouts  21.2 us (4%)
  blocking collectives  14.3 us (3%)
  between operations  14.3 us (3%)
    all_to_all x1, waiting for transfers between devices, per_device(): lax.all_to_all(grad_send, 'expert', split_axis=0, concat_axis=0, tiled=True)  84.7 us
    all_to_all x1, waiting for transfers between devices, per_device(): lax.all_to_all(partial_send, 'expert', split_axis=0, concat_axis=0, tiled...  82.4 us
    all_to_all x1, waiting for transfers between devices, per_device(): lax.all_to_all(place_rows(tokens), 'expert', split_axis=0, concat_axis=0,...  80.8 us
    all_to_all x1, waiting for transfers between devices, per_device(): lax.all_to_all(delta_send, 'expert', split_axis=0, concat_axis=0, tiled=T...  62.7 us
    psum x1, waiting for transfers between devices, backward_rows(): back_prop = lax.psum(back_prop, 'pipe')  37.2 us
    all_to_all x1, blocking collectives, per_device(): lax.all_to_all(fan_out(slot_gates), 'expert', split_axis=0, concat_axis=0...  14.3 us
    gather x2, local copies, waits for them, and re-layouts, gather_routes(): picked = jnp.take(row_table, flattened_index, axis=0)  13.4 us
    all_to_all x1, starting transfers between devices, per_device(): lax.all_to_all(grad_send, 'expert', split_axis=0, concat_axis=0, tiled=True)  13.3 us
  transfers between devices with their start and end apart: 5, of which 5 were waited for; matrix products, arithmetic and copies ran while one was open for 6% of the time, Pallas kernels for 0%

commit v1 on v0

v1 whole, which is shorter than its diff:
```python
import jax
import jax.numpy as jnp
from jax import lax
from jax.sharding import Mesh
from jax.sharding import PartitionSpec as P

GROUP = 8


beta_first = 0.9
beta_second = 0.95
learning_rate = 0.00022
decay_rate = 0.1
epsilon = 1e-08


def adamw(weight, moment_one, moment_two, gradient):
    weight_real = weight.astype(jnp.float32)
    first_new = beta_first * moment_one.astype(jnp.float32) + (1.0 - beta_first) * gradient
    second_new = (
        beta_second * moment_two.astype(jnp.float32) + (1.0 - beta_second) * gradient * gradient
    )
    weight_new = weight_real - learning_rate * (
        first_new / (jnp.sqrt(second_new) + epsilon) + decay_rate * weight_real
    )
    return (
        weight_new.astype(jnp.bfloat16),
        first_new.astype(jnp.bfloat16),
        second_new.astype(jnp.bfloat16),
    )


def f32_dot(left, right, dims):
    return lax.dot_general(left, right, (dims, ((), ())), preferred_element_type=jnp.float32)


def swap(value, axis):
    return lax.ppermute(value, axis, [(0, 1), (1, 0)])


def shift(value, step):
    size = lax.axis_size("x")
    return lax.ppermute(value, "x", [(i, (i + step) % size) for i in range(size)])


def to_bf16(value):
    return value.astype(jnp.bfloat16)


def per_device(
    tokens,
    grad_out,
    routed_expert_index,
    route_gates,
    gate_up,
    gate_up_m,
    gate_up_v,
    down,
    down_m,
    down_v,
):
    expert_list = lax.axis_size("y_lo") * lax.axis_size("z_hi")
    tok_dev, width_dev = tokens.shape
    hidden = gate_up.shape[2]
    capacity = 16
    rows = expert_list * capacity

    experts = jnp.arange(expert_list, dtype=jnp.int32)[:, None, None]
    index_t = routed_expert_index.T
    gates_t = route_gates.T.astype(jnp.float32)
    named = (index_t[None] == experts).astype(jnp.float32)
    member = jnp.sum(named, axis=1)
    gate_of = jnp.sum(named * gates_t[None], axis=1)
    earlier = (
        lax.broadcasted_iota(jnp.int32, (tok_dev, tok_dev), 0)
        < lax.broadcasted_iota(jnp.int32, (tok_dev, tok_dev), 1)
    ).astype(jnp.bfloat16)
    slot = f32_dot(to_bf16(member), earlier, ((1,), (0,))).astype(jnp.int32)
    slots = lax.broadcasted_iota(jnp.int32, (expert_list, capacity, tok_dev), 1)
    here = (slots == slot[:, None, :]) & (member[:, None, :] > 0.5)
    selector = here.astype(jnp.bfloat16).reshape(rows, tok_dev)
    gate_selector = to_bf16(jnp.where(here, gate_of[:, None, :], 0.0)).reshape(rows, tok_dev)

    tok_rows = to_bf16(f32_dot(selector, tokens, ((1,), (0,))))
    grad_rows = to_bf16(f32_dot(gate_selector, grad_out, ((1,), (0,))))
    send = jnp.concatenate(
        (
            tok_rows.reshape(expert_list, capacity, width_dev),
            grad_rows.reshape(expert_list, capacity, width_dev),
        ),
        axis=1,
    )
    got = lax.all_to_all(send, ("y_lo", "z_hi"), split_axis=0, concat_axis=0, tiled=True)
    tok_own = got[:, :capacity].reshape(rows, width_dev)
    grad_own = got[:, capacity:].reshape(rows, width_dev)

    paired_own = jnp.concatenate((gate_up[0], gate_up[1]), axis=1)
    paired_own, down_late, tok_own, grad_own = lax.optimization_barrier(
        (paired_own, down, tok_own, grad_own)
    )
    tok_left = shift(tok_own, 1)
    grad_right = shift(grad_own, -1)
    tok_right = shift(tok_own, -1)
    grad_left = shift(grad_own, 1)
    paired_far = swap(paired_own, "z_lo")
    down_far = swap(down_late, "z_lo")
    tok_across = shift(tok_left, 1)
    grad_across = shift(grad_right, -1)
    paired = jnp.concatenate((paired_own, paired_far), axis=1)
    downs = jnp.concatenate((down, down_far), axis=0)

    tok_all = jnp.concatenate((tok_own, tok_left, tok_right, tok_across), axis=0)
    grad_all = jnp.concatenate((grad_own, grad_left, grad_right, grad_across), axis=0)

    pre = jnp.concatenate(
        (f32_dot(tok_all, paired, ((1,), (0,))), f32_dot(grad_all, downs, ((1,), (1,)))), axis=1
    )
    core = lax.axis_index("core")
    y_hi = lax.axis_index("y_hi")
    half = pre.shape[0] // 2
    keep = jnp.where(core == 0, pre[:half], pre[half:])
    other = to_bf16(jnp.where(core == 0, pre[half:], pre[:half]))
    keep = keep + swap(other, "core").astype(jnp.float32)
    quarter = half // 2
    other = to_bf16(jnp.where(y_hi == 0, keep[quarter:], keep[:quarter]))
    keep = jnp.where(y_hi == 0, keep[:quarter], keep[quarter:])
    keep = keep + swap(other, "y_hi").astype(jnp.float32)

    def block(first):
        return jnp.concatenate(
            (keep[:, first : first + hidden], keep[:, first + 2 * hidden : first + 3 * hidden]),
            axis=1,
        )

    gate_pre = block(0)
    up_pre = block(hidden)
    back = keep[:, 4 * hidden :]
    sigmoid_gate = jax.nn.sigmoid(gate_pre)
    silu_gate = gate_pre * sigmoid_gate
    scaled = to_bf16(silu_gate * up_pre)
    d_gate = to_bf16(back * up_pre * sigmoid_gate * (1.0 + gate_pre * (1.0 - sigmoid_gate)))
    d_up = to_bf16(back * silu_gate)
    points = jnp.concatenate(
        (d_gate[:, :hidden], d_up[:, :hidden], d_gate[:, hidden:], d_up[:, hidden:], scaled), axis=1
    )
    far = swap(points, "y_hi")
    points = jnp.where(
        y_hi == 0, jnp.concatenate((points, far), axis=0), jnp.concatenate((far, points), axis=0)
    )
    far = swap(points, "core")
    points = jnp.where(
        core == 0, jnp.concatenate((points, far), axis=0), jnp.concatenate((far, points), axis=0)
    )
    d_paired = points[:, : 4 * hidden]
    scaled = points[:, 4 * hidden :]

    mixed_part = f32_dot(scaled, downs, ((1,), (0,)))
    delta_part = f32_dot(d_paired, paired, ((1,), (1,)))

    def part(value, chunk):
        return value[chunk * rows : (chunk + 1) * rows]

    mixed_in = shift(to_bf16(part(mixed_part, 3)), 1)
    delta_in = shift(to_bf16(part(delta_part, 3)), -1)
    mixed_b = shift(to_bf16(part(mixed_part, 1)), -1)
    delta_b = shift(to_bf16(part(delta_part, 2)), 1)
    mixed_a = shift(to_bf16(part(mixed_part, 2) + mixed_in.astype(jnp.float32)), 1)
    delta_a = shift(to_bf16(part(delta_part, 1) + delta_in.astype(jnp.float32)), -1)
    mixed_sum = to_bf16(
        part(mixed_part, 0) + mixed_a.astype(jnp.float32) + mixed_b.astype(jnp.float32)
    )
    delta_sum = to_bf16(
        part(delta_part, 0) + delta_a.astype(jnp.float32) + delta_b.astype(jnp.float32)
    )

    grad_paired_far = to_bf16(f32_dot(tok_all, d_paired[:, 2 * hidden :], ((0,), (0,))))
    grad_down_far = to_bf16(f32_dot(scaled[:, hidden:], grad_all, ((0,), (0,))))
    grad_paired_in = swap(grad_paired_far, "z_lo")
    grad_down_in = swap(grad_down_far, "z_lo")
    grad_paired = f32_dot(tok_all, d_paired[:, : 2 * hidden], ((0,), (0,)))
    grad_paired = grad_paired + grad_paired_in.astype(jnp.float32)
    grad_down = f32_dot(scaled[:, :hidden], grad_all, ((0,), (0,)))
    grad_down = grad_down + grad_down_in.astype(jnp.float32)
    grad_stack = jnp.stack((grad_paired[:, :hidden], grad_paired[:, hidden:]), axis=0)
    gate_up_new, gate_up_m_new, gate_up_v_new = adamw(gate_up, gate_up_m, gate_up_v, grad_stack)
    down_new, down_m_new, down_v_new = adamw(down, down_m, down_v, grad_down)

    back_send = jnp.concatenate(
        (
            mixed_sum.reshape(expert_list, capacity, width_dev),
            delta_sum.reshape(expert_list, capacity, width_dev),
        ),
        axis=1,
    )
    returned = lax.all_to_all(back_send, ("y_lo", "z_hi"), split_axis=0, concat_axis=0, tiled=True)
    mixed_rows = returned[:, :capacity].reshape(rows, width_dev)
    delta_rows = returned[:, capacity:].reshape(rows, width_dev)
    mixed = to_bf16(f32_dot(gate_selector, mixed_rows, ((0,), (0,))))
    grad_tokens = to_bf16(f32_dot(selector, delta_rows, ((0,), (0,))))
    return (
        mixed,
        grad_tokens,
        gate_up_new,
        gate_up_m_new,
        gate_up_v_new,
        down_new,
        down_m_new,
        down_v_new,
    )


def solution(mesh):
    pipe = ("y_hi", "core")
    expert = ("y_lo", "z_hi", "z_lo", "x")
    fine = Mesh(mesh.devices.reshape(2, 2, 2, 4, 2, 4), pipe + expert)
    rows_spec = P(expert, pipe)
    route_spec = P(expert, None)
    cols_spec = P(None, pipe, expert)
    return jax.shard_map(
        per_device,
        mesh=fine,
        in_specs=(
            rows_spec,
            rows_spec,
            route_spec,
            route_spec,
            cols_spec,
            cols_spec,
            cols_spec,
            rows_spec,
            rows_spec,
            rows_spec,
        ),
        out_specs=(
            rows_spec,
            rows_spec,
            cols_spec,
            cols_spec,
            cols_spec,
            rows_spec,
            rows_spec,
            rows_spec,
        ),
        check_vma=False,
    )
```

time: 480 us -> 177 us (0.37)
  the two profiles are of different devices: /device:TPU:6 before, /device:TPU:32 now
where the time goes in v1:
time: 177 us
  waiting for transfers between devices  106 us (60%)
  starting transfers between devices  37.2 us (21%)
  matrix products  17.6 us (10%)
  other arithmetic  10 us (6%)
  local copies, waits for them, and re-layouts  4.68 us (3%)
    ppermute x12, waiting for transfers between devices, shift(): lax.ppermute(value, 'x', [(i, (i + step) % size) for i in range(size)])  38.5 us
    ppermute x8, waiting for transfers between devices, swap(): return lax.ppermute(value, axis, [(0, 1), (1, 0)])  27.7 us
    all_to_all x1, waiting for transfers between devices, per_device(): lax.all_to_all(send, ('y_lo', 'z_hi'), split_axis=0, concat_axis=0, tiled...  25.5 us
    dot_general x13, matrix products, f32_dot(): lax.dot_general(left, right, (dims, ((), ())), preferred_element_type=jnp...  17.6 us
    ppermute x12, starting transfers between devices, shift(): lax.ppermute(value, 'x', [(i, (i + step) % size) for i in range(size)])  17.3 us
    all_to_all x1, waiting for transfers between devices, per_device(): lax.all_to_all(back_send, ('y_lo', 'z_hi'), split_axis=0, concat_axis=0,...  14.2 us
    all_to_all x1, starting transfers between devices, per_device(): lax.all_to_all(send, ('y_lo', 'z_hi'), split_axis=0, concat_axis=0, tiled...  8.71 us
    ppermute x8, starting transfers between devices, swap(): return lax.ppermute(value, axis, [(0, 1), (1, 0)])  6.84 us
  transfers between devices with their start and end apart: 22, of which 14 were waited for; matrix products, arithmetic and copies ran while one was open for 8% of the time, Pallas kernels for 0%

profile of v1, /device:TPU:32, one launch (start us, length us, event | category | flops | bytes accessed | tf_op | source)
XLA Modules:
  0.0 176.6 jit_solution(15686337604062580310)
XLA Ops:
  2.8 1.3 convolution_convert_fusion.3
  5.1 8.7 %all-to-all-start = ((bf16[8,32,1792]{2,1,0:T(8,128)(2,1)}), bf16[8,32,1792]{2,1,0:T(8,128)(2,1)S(1)}, u32[]{:S(2)}, u32[]{:S(2)}) async-start(bf16[8,32,1792]{2,1,0:T(8,128)(2,1)} %pad_maximum_fusion.2), calls=%async_computation | async-start | bytes 1835008 | tf_op jit(solution)/shard_map/all_to_all | solution.py:93
  14.8 25.5 %all-to-all-done = bf16[8,32,1792]{2,1,0:T(8,128)(2,1)S(1)} async-done(((bf16[8,32,1792]{2,1,0:T(8,128)(2,1)}), bf16[8,32,1792]{2,1,0:T(8,128)(2,1)S(1)}, u32[]{:S(2)}, u32[]{:S(2)}) %all-to-all-start) | async-done | bytes 917536 | tf_op jit(solution)/shard_map/all_to_all | solution.py:93
  40.3 1.6 collective-permute-start.4
  41.9 1.8 collective-permute-start.5
  43.9 3.0 %collective-permute-start.1 = (bf16[128,1792]{1,0:T(8,128)(2,1)S(1)}, bf16[128,1792]{1,0:T(8,128)(2,1)S(1)}, u32[]{:S(2)}, u32[]{:S(2)}) collective-permute-start(bf16[128,1792]{1,0:T(8,128)(2,1)S(1)} %bitcast.54), channel_id=1, source_target_pairs={{0,3},{1,0},{2,1},{3,2},{4,7},{5,4},{6,5},{7,6},{8,11},{9,8},{10,9... | collective-permute-start | bytes 1376264 | tf_op jit(solution)/shard_map/ppermute | solution.py:43
  47.1 8.0 %collective-permute-done.4 = bf16[128,1792]{1,0:T(8,128)(2,1)S(1)} collective-permute-done((bf16[128,1792]{1,0:T(8,128)(2,1)S(1)}, bf16[128,1792]{1,0:T(8,128)(2,1)S(1)}, u32[]{:S(2)}, u32[]{:S(2)}) %collective-permute-start.4) | collective-permute-done | bytes 458784 | tf_op jit(solution)/shard_map/ppermute | solution.py:43
  55.4 3.0 %collective-permute-start.6 = (bf16[128,1792]{1,0:T(8,128)(2,1)S(1)}, bf16[128,1792]{1,0:T(8,128)(2,1)S(1)}, u32[]{:S(2)}, u32[]{:S(2)}) collective-permute-start(bf16[128,1792]{1,0:T(8,128)(2,1)S(1)} %collective-permute-done.5), channel_id=1, source_target_pairs={{0,3},{1,0},{2,1},{3,2},{4,7},{5,4},{6,5},{7,6},{8,11},{9,8},{10,9... | collective-permute-start | bytes 1376264 | tf_op jit(solution)/shard_map/ppermute | solution.py:43
  58.3 4.0 %collective-permute-done = bf16[128,1792]{1,0:T(8,128)(2,1)S(1)} collective-permute-done((bf16[128,1792]{1,0:T(8,128)(2,1)S(1)}, bf16[128,1792]{1,0:T(8,128)(2,1)S(1)}, u32[]{:S(2)}, u32[]{:S(2)}) %collective-permute-start) | collective-permute-done | bytes 458784 | tf_op jit(solution)/shard_map/ppermute | solution.py:43
  62.7 13.6 %collective-permute-done.7 = bf16[128,1792]{1,0:T(8,128)(2,1)S(1)} collective-permute-done((bf16[128,1792]{1,0:T(8,128)(2,1)S(1)}, bf16[128,1792]{1,0:T(8,128)(2,1)S(1)}, u32[]{:S(2)}, u32[]{:S(2)}) %collective-permute-start.7) | collective-permute-done | bytes 458784 | tf_op jit(solution)/shard_map/ppermute | solution.py:38
  80.6 2.1 %collective-permute-done.8 = bf16[256,768]{0,1:T(8,128)(2,1)} collective-permute-done((bf16[256,768]{0,1:T(8,128)(2,1)}, bf16[256,768]{0,1:T(8,128)(2,1)}, u32[]{:S(2)}, u32[]{:S(2)}) %collective-permute-start.8) | collective-permute-done | bytes 393248 | tf_op jit(solution)/shard_map/ppermute | solution.py:38
  82.6 1.3 convert_add_fusion
  84.0 3.0 %collective-permute-start.9 = (bf16[128,768]{0,1:T(8,128)(2,1)S(1)}, bf16[128,768]{0,1:T(8,128)(2,1)S(1)}, u32[]{:S(2)}, u32[]{:S(2)}) collective-permute-start(bf16[128,768]{0,1:T(8,128)(2,1)S(1)} %select_convert_fusion.1), channel_id=1, source_target_pairs={{0,128},{128,0},{1,129},{129,1},{2,130},{130,2},{3,131},{131,3},{4... | collective-permute-start | bytes 589832 | tf_op jit(solution)/shard_map/ppermute | solution.py:38
  87.0 5.5 %collective-permute-done.9 = bf16[128,768]{0,1:T(8,128)(2,1)S(1)} collective-permute-done((bf16[128,768]{0,1:T(8,128)(2,1)S(1)}, bf16[128,768]{0,1:T(8,128)(2,1)S(1)}, u32[]{:S(2)}, u32[]{:S(2)}) %collective-permute-start.9) | collective-permute-done | bytes 196640 | tf_op jit(solution)/shard_map/ppermute | solution.py:38
  92.8 3.0 %collective-permute-start.10 = (bf16[128,768]{0,1:T(8,128)(2,1)S(1)}, bf16[128,768]{0,1:T(8,128)(2,1)S(1)}, u32[]{:S(2)}, u32[]{:S(2)}) collective-permute-start(bf16[128,768]{0,1:T(8,128)(2,1)S(1)} %fusion.32), channel_id=1, source_target_pairs={{0,128},{128,0},{1,129},{129,1},{2,130},{130,2},{3,131},{131,3},{4... | collective-permute-start | bytes 589832 | tf_op jit(solution)/shard_map/ppermute | solution.py:38
  95.8 4.7 %collective-permute-done.10 = bf16[128,768]{0,1:T(8,128)(2,1)S(1)} collective-permute-done((bf16[128,768]{0,1:T(8,128)(2,1)S(1)}, bf16[128,768]{0,1:T(8,128)(2,1)S(1)}, u32[]{:S(2)}, u32[]{:S(2)}) %collective-permute-start.10) | collective-permute-done | bytes 196640 | tf_op jit(solution)/shard_map/ppermute | solution.py:38
  101.0 1.7 collective-permute-done.11
  104.9 3.2 %collective-permute-start.15 = (bf16[128,1792]{1,0:T(8,128)(2,1)S(1)}, bf16[128,1792]{1,0:T(8,128)(2,1)S(1)}, u32[]{:S(2)}, u32[]{:S(2)}) collective-permute-start(bf16[128,1792]{1,0:T(8,128)(2,1)S(1)} %get-tuple-element.25), channel_id=1, source_target_pairs={{0,3},{1,0},{2,1},{3,2},{4,7},{5,4},{6,5},{7,6},{8,11},{9,8},{10,9... | collective-permute-start | bytes 1376264 | tf_op jit(solution)/shard_map/ppermute | solution.py:43
  108.3 2.0 %collective-permute-start.12 = (bf16[128,1792]{1,0:T(8,128)(2,1)S(1)}, bf16[128,1792]{1,0:T(8,128)(2,1)S(1)}, u32[]{:S(2)}, u32[]{:S(2)}) collective-permute-start(bf16[128,1792]{1,0:T(8,128)(2,1)S(1)} %get-tuple-element.23), channel_id=1, source_target_pairs={{0,1},{1,2},{2,3},{3,0},{4,5},{5,6},{6,7},{7,4},{8,9},{9,10},{10,1... | collective-permute-start | bytes 1376264 | tf_op jit(solution)/shard_map/ppermute | solution.py:43
  110.3 1.6 convolution_convert_fusion
  112.6 6.4 %collective-permute-done.15 = bf16[128,1792]{1,0:T(8,128)(2,1)S(1)} collective-permute-done((bf16[128,1792]{1,0:T(8,128)(2,1)S(1)}, bf16[128,1792]{1,0:T(8,128)(2,1)S(1)}, u32[]{:S(2)}, u32[]{:S(2)}) %collective-permute-start.15) | collective-permute-done | bytes 458784 | tf_op jit(solution)/shard_map/ppermute | solution.py:43
  119.4 9.1 %collective-permute-done.12 = bf16[128,1792]{1,0:T(8,128)(2,1)S(1)} collective-permute-done((bf16[128,1792]{1,0:T(8,128)(2,1)S(1)}, bf16[128,1792]{1,0:T(8,128)(2,1)S(1)}, u32[]{:S(2)}, u32[]{:S(2)}) %collective-permute-start.12) | collective-permute-done | bytes 458784 | tf_op jit(solution)/shard_map/ppermute | solution.py:43
  128.6 2.1 %collective-permute-start.13 = (bf16[128,1792]{1,0:T(8,128)(2,1)S(1)}, bf16[128,1792]{1,0:T(8,128)(2,1)S(1)}, u32[]{:S(2)}, u32[]{:S(2)}) collective-permute-start(bf16[128,1792]{1,0:T(8,128)(2,1)S(1)} %fusion.13), channel_id=1, source_target_pairs={{0,1},{1,2},{2,3},{3,0},{4,5},{5,6},{6,7},{7,4},{8,9},{9,10},{10,1... | collective-permute-start | bytes 1376264 | tf_op jit(solution)/shard_map/ppermute | solution.py:43
  130.7 9.5 %collective-permute-done.16 = bf16[128,1792]{1,0:T(8,128)(2,1)S(1)} collective-permute-done((bf16[128,1792]{1,0:T(8,128)(2,1)S(1)}, bf16[128,1792]{1,0:T(8,128)(2,1)S(1)}, u32[]{:S(2)}, u32[]{:S(2)}) %collective-permute-start.16) | collective-permute-done | bytes 458784 | tf_op jit(solution)/shard_map/ppermute | solution.py:43
  140.4 1.2 collective-permute-done.13
  142.8 4.4 %all-to-all-start.1 = ((bf16[8,32,1792]{2,1,0:T(8,128)(2,1)}), bf16[8,32,1792]{2,1,0:T(8,128)(2,1)}, u32[]{:S(2)}, u32[]{:S(2)}) async-start(bf16[8,32,1792]{2,1,0:T(8,128)(2,1)} %pad_maximum_fusion.3), calls=%async_computation.1 | async-start | bytes 1835008 | tf_op jit(solution)/shard_map/all_to_all | solution.py:195
  147.2 4.1 %fusion.22 = (bf16[128,1792]{1,0:T(8,128)(2,1)}, bf16[128,1792]{1,0:T(8,128)(2,1)}, bf16[128,1792]{1,0:T(8,128)(2,1)}) fusion(bf16[128,1792]{1,0:T(8,128)(2,1)} %param.19, bf16[128,1792]{1,0:T(8,128)(2,1)} %param.18, bf16[128,1792]{1,0:T(8,128)(2,1)} %param.17, bf16[128,1792]{1,0:T(8,128)(2,1)} %collective-permute-done.19, bf16[512,1792]{1,0:T(8,128)(2,1)} %copy-done.5, ...), kind=kOutput, calls=%fused_computation.55 | convolution fusion | flops 239697920 | bytes 5177344 | tf_op jit(solution)/shard_map/dot_general | solution.py:34
  151.4 1.9 %convolution_add_fusion = f32[1792,256]{1,0:T(8,128)S(1)} fusion(bf16[512,1792]{1,0:T(8,128)(2,1)S(1)} %constant_dynamic-update-slice_fusion, bf16[1792,256]{1,0:T(8,128)(2,1)} %collective-permute-done.18, bf16[512,768]{0,1:T(8,128)(2,1)S(1)} %maximum_select_fusion), kind=kOutput, calls=%fused_computation | convolution fusion | flops 470679552 | bytes 4849664 | tf_op jit(solution)/shard_map/dot_general | solution.py:34
  155.0 3.1 %fusion.18 = (bf16[2,1792,128]{2,1,0:T(8,128)(2,1)}, bf16[2,1792,128]{2,1,0:T(8,128)(2,1)}, bf16[2,1792,128]{2,1,0:T(8,128)(2,1)}) fusion(f32[1,1792,128]{2,1,0:T(8,128)S(1)} %get-tuple-element.22, f32[1,1792,128]{2,1,0:T(8,128)S(1)} %get-tuple-element.21, bf16[2,1792,128]{2,1,0:T(8,128)(2,1)S(1)} %copy-done.11, bf16[2,1792,128]{2,1,0:T(8,128)(2,1)S(1)} %copy-done.12, ...), kind=kLoop, calls=%fused_computation.51 | loop fusion | flops 9175040 | bytes 7340032 | tf_op jit(solution)/shard_map/convert_element_type | solution.py:29
  158.1 14.2 %all-to-all-done.1 = bf16[8,32,1792]{2,1,0:T(8,128)(2,1)} async-done(((bf16[8,32,1792]{2,1,0:T(8,128)(2,1)}), bf16[8,32,1792]{2,1,0:T(8,128)(2,1)}, u32[]{:S(2)}, u32[]{:S(2)}) %all-to-all-start.1) | async-done | bytes 917536 | tf_op jit(solution)/shard_map/all_to_all | solution.py:195
  172.3 2.1 %fusion = bf16[128,1792]{1,0:T(8,128)(2,1)} fusion(bf16[8,32,1792]{2,1,0:T(8,128)(2,1)} %all-to-all-done.1, bf16[8,128]{1,0:T(8,128)(2,1)S(1)} %get-tuple-element.17, s32[8,128]{1,0:T(8,128)S(1)} %convolution_convert_fusion.4, pred[8,128]{1,0:T(8,128)(4,1)S(1)} %broadcast_compare_fusion), kind=kOutput, calls=%fused_computation.6 | convolution fusion | flops 58998784 | bytes 924672 | tf_op jit(solution)/shard_map/dot_general | solution.py:34
  174.4 2.1 %fusion.1 = bf16[128,1792]{1,0:T(8,128)(2,1)} fusion(bf16[8,32,1792]{2,1,0:T(8,128)(2,1)} %all-to-all-done.1, s32[8,128]{1,0:T(8,128)S(1)} %convolution_convert_fusion.4, pred[8,128]{1,0:T(8,128)(4,1)S(1)} %broadcast_compare_fusion), kind=kOutput, calls=%fused_computation.7 | convolution fusion | flops 58982400 | bytes 922624 | tf_op jit(solution)/shard_map/dot_general | solution.py:34
  (99 shorter events, 16.6 us)
Async XLA Ops:
  0.6 1.9 %copy-start = (bf16[128,1792]{1,0:T(8,128)(2,1)S(1)}, bf16[128,1792]{1,0:T(8,128)(2,1)}, u32[]{:S(2)}) copy-start(bf16[128,1792]{1,0:T(8,128)(2,1)} %param.11) | copy-start | bytes 1376260
  4.1 9.7 %copy-start.13 = (bf16[128,1792]{1,0:T(8,128)(2,1)S(1)}, bf16[128,1792]{1,0:T(8,128)(2,1)}, u32[]{:S(2)}) copy-start(bf16[128,1792]{1,0:T(8,128)(2,1)} %param.17) | copy-start | bytes 1376260
  5.1 9.5 %copy-start.3 = (bf16[2,1792,128]{2,1,0:T(8,128)(2,1)S(1)}, bf16[2,1792,128]{2,1,0:T(8,128)(2,1)}, u32[]{:S(2)}) copy-start(bf16[2,1792,128]{2,1,0:T(8,128)(2,1)} %param.14) | copy-start | bytes 2752516
  5.1 35.1 %all-to-all-start = ((bf16[8,32,1792]{2,1,0:T(8,128)(2,1)}), bf16[8,32,1792]{2,1,0:T(8,128)(2,1)S(1)}, u32[]{:S(2)}, u32[]{:S(2)}) async-start(bf16[8,32,1792]{2,1,0:T(8,128)(2,1)} %pad_maximum_fusion.2), calls=%async_computation | async-start | bytes 1835008 | tf_op jit(solution)/shard_map/all_to_all | solution.py:93
  40.3 14.8 %copy-start.14 = (bf16[128,1792]{1,0:T(8,128)(2,1)S(1)}, bf16[128,1792]{1,0:T(8,128)(2,1)}, u32[]{:S(2)}) copy-start(bf16[128,1792]{1,0:T(8,128)(2,1)} %param.17) | copy-start | bytes 1376260
  40.3 14.7 %collective-permute-start.4 = (bf16[128,1792]{1,0:T(8,128)(2,1)S(1)}, bf16[128,1792]{1,0:T(8,128)(2,1)S(1)}, u32[]{:S(2)}, u32[]{:S(2)}) collective-permute-start(bf16[128,1792]{1,0:T(8,128)(2,1)S(1)} %bitcast.56), channel_id=1, source_target_pairs={{0,1},{1,2},{2,3},{3,0},{4,5},{5,6},{6,7},{7,4},{8,9},{9,10},{10,1... | collective-permute-start | bytes 1376264 | tf_op jit(solution)/shard_map/ppermute | solution.py:43
  41.9 13.5 %collective-permute-start.5 = (bf16[128,1792]{1,0:T(8,128)(2,1)S(1)}, bf16[128,1792]{1,0:T(8,128)(2,1)S(1)}, u32[]{:S(2)}, u32[]{:S(2)}) collective-permute-start(bf16[128,1792]{1,0:T(8,128)(2,1)S(1)} %bitcast.57), channel_id=1, source_target_pairs={{0,3},{1,0},{2,1},{3,2},{4,7},{5,4},{6,5},{7,6},{8,11},{9,8},{10,9... | collective-permute-start | bytes 1376264 | tf_op jit(solution)/shard_map/ppermute | solution.py:43
  43.7 18.7 %collective-permute-start = (bf16[128,1792]{1,0:T(8,128)(2,1)S(1)}, bf16[128,1792]{1,0:T(8,128)(2,1)S(1)}, u32[]{:S(2)}, u32[]{:S(2)}) collective-permute-start(bf16[128,1792]{1,0:T(8,128)(2,1)S(1)} %bitcast.53), channel_id=1, source_target_pairs={{0,1},{1,2},{2,3},{3,0},{4,5},{5,6},{6,7},{7,4},{8,9},{9,10},{10,1... | collective-permute-start | bytes 1376264 | tf_op jit(solution)/shard_map/ppermute | solution.py:43
  43.9 32.4 %collective-permute-start.1 = (bf16[128,1792]{1,0:T(8,128)(2,1)S(1)}, bf16[128,1792]{1,0:T(8,128)(2,1)S(1)}, u32[]{:S(2)}, u32[]{:S(2)}) collective-permute-start(bf16[128,1792]{1,0:T(8,128)(2,1)S(1)} %bitcast.54), channel_id=1, source_target_pairs={{0,3},{1,0},{2,1},{3,2},{4,7},{5,4},{6,5},{7,6},{8,11},{9,8},{10,9... | collective-permute-start | bytes 1376264 | tf_op jit(solution)/shard_map/ppermute | solution.py:43
  46.9 29.5 %collective-permute-start.3 = (bf16[1792,256]{1,0:T(8,128)(2,1)S(1)}, bf16[1792,256]{1,0:T(8,128)(2,1)S(1)}, u32[]{:S(2)}, u32[]{:S(2)}) collective-permute-start(bf16[1792,256]{1,0:T(8,128)(2,1)S(1)} %pad_maximum_fusion.1), channel_id=1, source_target_pairs={{0,4},{4,0},{1,5},{5,1},{2,6},{6,2},{3,7},{7,3},{8,12},{12,8},{9,1... | collective-permute-start | bytes 2752520 | tf_op jit(solution)/shard_map/ppermute | solution.py:38
  47.0 29.3 %copy-start.8 = (bf16[256,1792]{1,0:T(8,128)(2,1)S(1)}, bf16[256,1792]{1,0:T(8,128)(2,1)}, u32[]{:S(2)}) copy-start(bf16[256,1792]{1,0:T(8,128)(2,1)} %constant_dynamic-update-slice_fusion.11) | copy-start | bytes 2752516
  55.1 21.2 %collective-permute-start.7 = (bf16[128,1792]{1,0:T(8,128)(2,1)S(1)}, bf16[128,1792]{1,0:T(8,128)(2,1)S(1)}, u32[]{:S(2)}, u32[]{:S(2)}) collective-permute-start(bf16[128,1792]{1,0:T(8,128)(2,1)S(1)} %copy-done.14), channel_id=1, source_target_pairs={{0,4},{4,0},{1,5},{5,1},{2,6},{6,2},{3,7},{7,3},{8,12},{12,8},{9,1... | collective-permute-start | bytes 1376264 | tf_op jit(solution)/shard_map/ppermute | solution.py:38
  55.4 21.1 %collective-permute-start.6 = (bf16[128,1792]{1,0:T(8,128)(2,1)S(1)}, bf16[128,1792]{1,0:T(8,128)(2,1)S(1)}, u32[]{:S(2)}, u32[]{:S(2)}) collective-permute-start(bf16[128,1792]{1,0:T(8,128)(2,1)S(1)} %collective-permute-done.5), channel_id=1, source_target_pairs={{0,3},{1,0},{2,1},{3,2},{4,7},{5,4},{6,5},{7,6},{8,11},{9,8},{10,9... | collective-permute-start | bytes 1376264 | tf_op jit(solution)/shard_map/ppermute | solution.py:43
  62.3 16.2 %collective-permute-start.2 = (bf16[128,1792]{1,0:T(8,128)(2,1)S(1)}, bf16[128,1792]{1,0:T(8,128)(2,1)S(1)}, u32[]{:S(2)}, u32[]{:S(2)}) collective-permute-start(bf16[128,1792]{1,0:T(8,128)(2,1)S(1)} %collective-permute-done), channel_id=1, source_target_pairs={{0,1},{1,2},{2,3},{3,0},{4,5},{5,6},{6,7},{7,4},{8,9},{9,10},{10,1... | collective-permute-start | bytes 1376264 | tf_op jit(solution)/shard_map/ppermute | solution.py:43
  76.5 2.1 %copy-start.1 = (bf16[1792,512]{1,0:T(8,128)(2,1)}, bf16[1792,512]{1,0:T(8,128)(2,1)S(1)}, u32[]{:S(2)}) copy-start(bf16[1792,512]{1,0:T(8,128)(2,1)S(1)} %constant_dynamic-update-slice_fusion.4) | copy-start | bytes 5505028
  80.6 2.1 %collective-permute-start.8 = (bf16[256,768]{0,1:T(8,128)(2,1)}, bf16[256,768]{0,1:T(8,128)(2,1)}, u32[]{:S(2)}, u32[]{:S(2)}) collective-permute-start(bf16[256,768]{0,1:T(8,128)(2,1)} %select_convert_fusion), channel_id=1, source_target_pairs={{0,64},{64,0},{1,65},{65,1},{2,66},{66,2},{3,67},{67,3},{4,68},{68... | collective-permute-start | bytes 1179656 | tf_op jit(solution)/shard_map/ppermute | solution.py:38
  84.0 8.5 %collective-permute-start.9 = (bf16[128,768]{0,1:T(8,128)(2,1)S(1)}, bf16[128,768]{0,1:T(8,128)(2,1)S(1)}, u32[]{:S(2)}, u32[]{:S(2)}) collective-permute-start(bf16[128,768]{0,1:T(8,128)(2,1)S(1)} %select_convert_fusion.1), channel_id=1, source_target_pairs={{0,128},{128,0},{1,129},{129,1},{2,130},{130,2},{3,131},{131,3},{4... | collective-permute-start | bytes 589832 | tf_op jit(solution)/shard_map/ppermute | solution.py:38
  92.6 10.3 %copy-start.2 = (bf16[1792,512]{1,0:T(8,128)(2,1)S(1)}, bf16[1792,512]{1,0:T(8,128)(2,1)}, u32[]{:S(2)}) copy-start(bf16[1792,512]{1,0:T(8,128)(2,1)} %copy-done.1) | copy-start | bytes 5505028
  92.8 7.7 %collective-permute-start.10 = (bf16[128,768]{0,1:T(8,128)(2,1)S(1)}, bf16[128,768]{0,1:T(8,128)(2,1)S(1)}, u32[]{:S(2)}, u32[]{:S(2)}) collective-permute-start(bf16[128,768]{0,1:T(8,128)(2,1)S(1)} %fusion.32), channel_id=1, source_target_pairs={{0,128},{128,0},{1,129},{129,1},{2,130},{130,2},{3,131},{131,3},{4... | collective-permute-start | bytes 589832 | tf_op jit(solution)/shard_map/ppermute | solution.py:38
  100.7 2.0 %collective-permute-start.11 = (bf16[256,768]{0,1:T(8,128)(2,1)S(1)}, bf16[256,768]{0,1:T(8,128)(2,1)S(1)}, u32[]{:S(2)}, u32[]{:S(2)}) collective-permute-start(bf16[256,768]{0,1:T(8,128)(2,1)S(1)} %maximum_select_fusion.1), channel_id=1, source_target_pairs={{0,64},{64,0},{1,65},{65,1},{2,66},{66,2},{3,67},{67,3},{4,68},{68... | collective-permute-start | bytes 1179656 | tf_op jit(solution)/shard_map/ppermute | solution.py:38
  104.8 23.8 %collective-permute-start.17 = (bf16[128,1792]{1,0:T(8,128)(2,1)S(1)}, bf16[128,1792]{1,0:T(8,128)(2,1)S(1)}, u32[]{:S(2)}, u32[]{:S(2)}) collective-permute-start(bf16[128,1792]{1,0:T(8,128)(2,1)S(1)} %get-tuple-element.26), channel_id=1, source_target_pairs={{0,1},{1,2},{2,3},{3,0},{4,5},{5,6},{6,7},{7,4},{8,9},{9,10},{10,1... | collective-permute-start | bytes 1376264 | tf_op jit(solution)/shard_map/ppermute | solution.py:43
  104.9 14.1 %collective-permute-start.15 = (bf16[128,1792]{1,0:T(8,128)(2,1)S(1)}, bf16[128,1792]{1,0:T(8,128)(2,1)S(1)}, u32[]{:S(2)}, u32[]{:S(2)}) collective-permute-start(bf16[128,1792]{1,0:T(8,128)(2,1)S(1)} %get-tuple-element.25), channel_id=1, source_target_pairs={{0,3},{1,0},{2,1},{3,2},{4,7},{5,4},{6,5},{7,6},{8,11},{9,8},{10,9... | collective-permute-start | bytes 1376264 | tf_op jit(solution)/shard_map/ppermute | solution.py:43
  108.2 32.2 %collective-permute-start.14 = (bf16[128,1792]{1,0:T(8,128)(2,1)S(1)}, bf16[128,1792]{1,0:T(8,128)(2,1)S(1)}, u32[]{:S(2)}, u32[]{:S(2)}) collective-permute-start(bf16[128,1792]{1,0:T(8,128)(2,1)S(1)} %get-tuple-element.24), channel_id=1, source_target_pairs={{0,3},{1,0},{2,1},{3,2},{4,7},{5,4},{6,5},{7,6},{8,11},{9,8},{10,9... | collective-permute-start | bytes 1376264 | tf_op jit(solution)/shard_map/ppermute | solution.py:43
  108.3 3.9 %copy-start.6 = (bf16[512,1792]{1,0:T(8,128)(2,1)S(1)}, bf16[512,1792]{1,0:T(8,128)(2,1)}, u32[]{:S(2)}) copy-start(bf16[512,1792]{1,0:T(8,128)(2,1)} %copy-done.5) | copy-start | bytes 5505028
  108.3 20.2 %collective-permute-start.12 = (bf16[128,1792]{1,0:T(8,128)(2,1)S(1)}, bf16[128,1792]{1,0:T(8,128)(2,1)S(1)}, u32[]{:S(2)}, u32[]{:S(2)}) collective-permute-start(bf16[128,1792]{1,0:T(8,128)(2,1)S(1)} %get-tuple-element.23), channel_id=1, source_target_pairs={{0,1},{1,2},{2,3},{3,0},{4,5},{5,6},{6,7},{7,4},{8,9},{9,10},{10,1... | collective-permute-start | bytes 1376264 | tf_op jit(solution)/shard_map/ppermute | solution.py:43
  111.9 39.5 %collective-permute-start.18 = (bf16[1792,256]{1,0:T(8,128)(2,1)}, bf16[1792,256]{1,0:T(8,128)(2,1)}, u32[]{:S(2)}, u32[]{:S(2)}) collective-permute-start(bf16[1792,256]{1,0:T(8,128)(2,1)} %convolution_convert_fusion), channel_id=1, source_target_pairs={{0,4},{4,0},{1,5},{5,1},{2,6},{6,2},{3,7},{7,3},{8,12},{12,8},{9,1... | collective-permute-start | bytes 2752520 | tf_op jit(solution)/shard_map/ppermute | solution.py:38
  119.0 28.2 %collective-permute-start.19 = (bf16[128,1792]{1,0:T(8,128)(2,1)S(1)}, bf16[128,1792]{1,0:T(8,128)(2,1)}, u32[]{:S(2)}, u32[]{:S(2)}) collective-permute-start(bf16[128,1792]{1,0:T(8,128)(2,1)S(1)} %convolution_convert_fusion.1), channel_id=1, source_target_pairs={{0,4},{4,0},{1,5},{5,1},{2,6},{6,2},{3,7},{7,3},{8,12},{12,8},{9,1... | collective-permute-start | bytes 1376264 | tf_op jit(solution)/shard_map/ppermute | solution.py:38
  128.5 11.7 %collective-permute-start.16 = (bf16[128,1792]{1,0:T(8,128)(2,1)S(1)}, bf16[128,1792]{1,0:T(8,128)(2,1)S(1)}, u32[]{:S(2)}, u32[]{:S(2)}) collective-permute-start(bf16[128,1792]{1,0:T(8,128)(2,1)S(1)} %fusion.10), channel_id=1, source_target_pairs={{0,3},{1,0},{2,1},{3,2},{4,7},{5,4},{6,5},{7,6},{8,11},{9,8},{10,9... | collective-permute-start | bytes 1376264 | tf_op jit(solution)/shard_map/ppermute | solution.py:43
  128.6 13.0 %collective-permute-start.13 = (bf16[128,1792]{1,0:T(8,128)(2,1)S(1)}, bf16[128,1792]{1,0:T(8,128)(2,1)S(1)}, u32[]{:S(2)}, u32[]{:S(2)}) collective-permute-start(bf16[128,1792]{1,0:T(8,128)(2,1)S(1)} %fusion.13), channel_id=1, source_target_pairs={{0,1},{1,2},{2,3},{3,0},{4,5},{5,6},{6,7},{7,4},{8,9},{9,10},{10,1... | collective-permute-start | bytes 1376264 | tf_op jit(solution)/shard_map/ppermute | solution.py:43
  142.8 29.5 %all-to-all-start.1 = ((bf16[8,32,1792]{2,1,0:T(8,128)(2,1)}), bf16[8,32,1792]{2,1,0:T(8,128)(2,1)}, u32[]{:S(2)}, u32[]{:S(2)}) async-start(bf16[8,32,1792]{2,1,0:T(8,128)(2,1)} %pad_maximum_fusion.3), calls=%async_computation.1 | async-start | bytes 1835008 | tf_op jit(solution)/shard_map/all_to_all | solution.py:195
  153.3 1.4 copy-start.11
  153.3 1.7 copy-start.12
  (5 other events, 5.8 us)

commit v2 on v1

v2 whole, which is shorter than its diff:
```python
import jax
import jax.numpy as jnp
from jax import lax
from jax.sharding import Mesh
from jax.sharding import PartitionSpec as P


beta_first = 0.9
beta_second = 0.95
learning_rate = 0.00022
decay_rate = 0.1
epsilon = 1e-08


def adamw(weight, moment_one, moment_two, gradient):
    weight_real = weight.astype(jnp.float32)
    first_new = beta_first * moment_one.astype(jnp.float32) + (1.0 - beta_first) * gradient
    second_new = (
        beta_second * moment_two.astype(jnp.float32) + (1.0 - beta_second) * gradient * gradient
    )
    weight_new = weight_real - learning_rate * (
        first_new / (jnp.sqrt(second_new) + epsilon) + decay_rate * weight_real
    )
    return (
        weight_new.astype(jnp.bfloat16),
        first_new.astype(jnp.bfloat16),
        second_new.astype(jnp.bfloat16),
    )


def f32_dot(left, right, dims):
    return lax.dot_general(left, right, (dims, ((), ())), preferred_element_type=jnp.float32)


def swap(value, axis):
    return lax.ppermute(value, axis, [(0, 1), (1, 0)])


def shift(value, step):
    size = lax.axis_size("x")
    return lax.ppermute(value, "x", [(i, (i + step) % size) for i in range(size)])


def after(value, *earlier):
    return lax.optimization_barrier((value,) + earlier)[0]


def to_bf16(value):
    return value.astype(jnp.bfloat16)


def per_device(
    tokens,
    grad_out,
    routed_expert_index,
    route_gates,
    gate_up,
    gate_up_m,
    gate_up_v,
    down,
    down_m,
    down_v,
):
    expert_list = lax.axis_size("y_lo") * lax.axis_size("z_hi")
    tok_dev, width_dev = tokens.shape
    hidden = gate_up.shape[2]
    capacity = 16
    rows = expert_list * capacity

    experts = jnp.arange(expert_list, dtype=jnp.int32)[:, None, None]
    index_t = routed_expert_index.T
    gates_t = route_gates.T.astype(jnp.float32)
    named = (index_t[None] == experts).astype(jnp.float32)
    member = jnp.sum(named, axis=1)
    gate_of = jnp.sum(named * gates_t[None], axis=1)
    earlier = (
        lax.broadcasted_iota(jnp.int32, (tok_dev, tok_dev), 0)
        < lax.broadcasted_iota(jnp.int32, (tok_dev, tok_dev), 1)
    ).astype(jnp.bfloat16)
    slot = f32_dot(to_bf16(member), earlier, ((1,), (0,))).astype(jnp.int32)
    slots = lax.broadcasted_iota(jnp.int32, (expert_list, capacity, tok_dev), 1)
    here = (slots == slot[:, None, :]) & (member[:, None, :] > 0.5)
    selector = here.astype(jnp.bfloat16).reshape(rows, tok_dev)
    gate_selector = to_bf16(jnp.where(here, gate_of[:, None, :], 0.0)).reshape(rows, tok_dev)

    core = lax.axis_index("core")
    y_hi = lax.axis_index("y_hi")
    mid = rows // 2

    def exchange(first, second):
        pair = jnp.concatenate(
            (
                first.reshape(expert_list, capacity, width_dev),
                second.reshape(expert_list, capacity, width_dev),
            ),
            axis=1,
        )
        return lax.all_to_all(pair, ("y_lo", "z_hi"), split_axis=0, concat_axis=0, tiled=True)

    def core_sum(low, high):
        keep = jnp.where(core == 0, low, high)
        return keep + swap(jnp.where(core == 0, high, low), "core")

    def y_sum(keep):
        return keep + swap(to_bf16(keep), "y_hi").astype(jnp.float32)

    def core_gather(points):
        far = swap(points, "core")
        return jnp.where(
            core == 0,
            jnp.concatenate((points, far), axis=0),
            jnp.concatenate((far, points), axis=0),
        )

    def both(value, first):
        return jnp.concatenate(
            (value[:, first : first + hidden], value[:, first + 2 * hidden : first + 3 * hidden]),
            axis=1,
        )

    nothing = jnp.zeros_like(here, dtype=jnp.bfloat16)
    sel3 = here.astype(jnp.bfloat16)
    gate3 = gate_selector.reshape(sel3.shape)
    combine = jnp.concatenate(
        (
            jnp.concatenate((gate3, nothing), axis=2),
            jnp.concatenate((nothing, sel3), axis=2),
        ),
        axis=1,
    ).reshape(2 * rows, 2 * tok_dev)

    tok_rows = to_bf16(f32_dot(selector, tokens, ((1,), (0,))))
    grad_rows = to_bf16(f32_dot(gate_selector, grad_out, ((1,), (0,))))
    got = exchange(tok_rows, grad_rows)
    tok_own = got[:, :capacity].reshape(rows, width_dev)
    grad_own = got[:, capacity:].reshape(rows, width_dev)
    tok_own, grad_own, gate, up, down_late, combine = lax.optimization_barrier(
        (tok_own, grad_own, gate_up[0], gate_up[1], down, combine)
    )
    paired_own = jnp.concatenate((gate, up), axis=1)
    tok_left = shift(tok_own, 1)
    tok_right = shift(tok_own, -1)
    paired_far = swap(paired_own, "z_lo")
    tok_across = shift(tok_left, 1)
    grad_right = shift(after(grad_own, tok_right), -1)
    grad_left = shift(after(grad_own, tok_left), 1)
    grad_across = shift(grad_right, -1)
    down_far = swap(down_late, "z_lo")
    paired = jnp.concatenate((paired_own, paired_far), axis=1)
    downs = jnp.concatenate((down, down_far), axis=0)
    tok_low = jnp.concatenate((tok_own, tok_left), axis=0)
    tok_high = jnp.concatenate((tok_right, tok_across), axis=0)
    grad_low = jnp.concatenate((grad_own, grad_left), axis=0)
    grad_high = jnp.concatenate((grad_right, grad_across), axis=0)
    tok_all = jnp.concatenate((tok_low, tok_high), axis=0)
    grad_all = jnp.concatenate((grad_low, grad_high), axis=0)

    pre = y_sum(
        core_sum(
            f32_dot(tok_low, paired, ((1,), (0,))), f32_dot(tok_high, paired, ((1,), (0,)))
        )
    )
    gate_pre = both(pre, 0)
    up_pre = both(pre, hidden)
    sigmoid_gate = jax.nn.sigmoid(gate_pre)
    silu_gate = gate_pre * sigmoid_gate
    scaled = core_gather(to_bf16(silu_gate * up_pre))

    def scatter_x(value, step):
        chunks = [value[i * rows : (i + 1) * rows] for i in range(4)]
        near, back_near = (chunks[2], chunks[1]) if step == 1 else (chunks[1], chunks[2])
        across = shift(to_bf16(chunks[3]), step).astype(jnp.float32)
        other = shift(to_bf16(back_near), -step).astype(jnp.float32)
        one = shift(to_bf16(near + across), step).astype(jnp.float32)
        return to_bf16(chunks[0] + one + other)

    mixed_part = f32_dot(scaled, downs, ((1,), (0,)))
    mixed_sum = scatter_x(mixed_part, 1)

    grad_low = after(grad_low, scaled)
    back = y_sum(
        core_sum(f32_dot(grad_low, downs, ((1,), (1,))), f32_dot(grad_high, downs, ((1,), (1,))))
    )
    back, up_pre, gate_pre = lax.optimization_barrier((back, up_pre, gate_pre))
    sigmoid_gate = jax.nn.sigmoid(gate_pre)
    silu_gate = gate_pre * sigmoid_gate
    d_gate = to_bf16(back * up_pre * sigmoid_gate * (1.0 + gate_pre * (1.0 - sigmoid_gate)))
    d_up = to_bf16(back * silu_gate)
    d_paired = core_gather(
        jnp.concatenate(
            (d_gate[:, :hidden], d_up[:, :hidden], d_gate[:, hidden:], d_up[:, hidden:]), axis=1
        )
    )
    delta_sum = scatter_x(f32_dot(d_paired, paired, ((1,), (1,))), -1)
    returned = exchange(mixed_sum, delta_sum)

    grad_down_far = to_bf16(f32_dot(scaled[:, hidden:], grad_all, ((0,), (0,))))
    grad_down_in = swap(grad_down_far, "z_lo")
    grad_paired_far = to_bf16(f32_dot(tok_all, d_paired[:, 2 * hidden :], ((0,), (0,))))
    grad_paired_in = swap(grad_paired_far, "z_lo")
    grad_paired = f32_dot(tok_all, d_paired[:, : 2 * hidden], ((0,), (0,)))
    grad_paired = grad_paired + grad_paired_in.astype(jnp.float32)
    grad_down = f32_dot(scaled[:, :hidden], grad_all, ((0,), (0,)))
    grad_down = grad_down + grad_down_in.astype(jnp.float32)
    grad_stack = jnp.stack((grad_paired[:, :hidden], grad_paired[:, hidden:]), axis=0)
    gate_up_new, gate_up_m_new, gate_up_v_new = adamw(gate_up, gate_up_m, gate_up_v, grad_stack)
    down_new, down_m_new, down_v_new = adamw(down, down_m, down_v, grad_down)

    combined = to_bf16(
        f32_dot(combine, returned.reshape(2 * rows, width_dev), ((0,), (0,)))
    )
    mixed = combined[:tok_dev]
    grad_tokens = combined[tok_dev:]
    return (
        mixed,
        grad_tokens,
        gate_up_new,
        gate_up_m_new,
        gate_up_v_new,
        down_new,
        down_m_new,
        down_v_new,
    )


def solution(mesh):
    pipe = ("y_hi", "core")
    expert = ("y_lo", "z_hi", "z_lo", "x")
    fine = Mesh(mesh.devices.reshape(2, 2, 2, 4, 2, 4), pipe + expert)
    rows_spec = P(expert, pipe)
    route_spec = P(expert, None)
    cols_spec = P(None, pipe, expert)
    return jax.shard_map(
        per_device,
        mesh=fine,
        in_specs=(
            rows_spec,
            rows_spec,
            route_spec,
            route_spec,
            cols_spec,
            cols_spec,
            cols_spec,
            rows_spec,
            rows_spec,
            rows_spec,
        ),
        out_specs=(
            rows_spec,
            rows_spec,
            cols_spec,
            cols_spec,
            cols_spec,
            rows_spec,
            rows_spec,
            rows_spec,
        ),
        check_vma=False,
    )
```

time: 177 us -> 161 us (0.910)
  the two profiles are of different devices: /device:TPU:32 before, /device:TPU:6 now
where the time goes in v2:
time: 161 us; the launch traced here: 160 us
  waiting for transfers between devices  83.1 us (52%)
  starting transfers between devices  46.4 us (29%)
  matrix products  15 us (9%)
  other arithmetic  9.03 us (6%)
  local copies, waits for them, and re-layouts  5.64 us (4%)
    all_to_all x2, waiting for transfers between devices, exchange(): lax.all_to_all(pair, ('y_lo', 'z_hi'), split_axis=0, concat_axis=0, tiled...  28.8 us
    ppermute x12, waiting for transfers between devices, shift(): lax.ppermute(value, 'x', [(i, (i + step) % size) for i in range(size)])  27.9 us
    ppermute x10, waiting for transfers between devices, swap(): return lax.ppermute(value, axis, [(0, 1), (1, 0)])  26.3 us
    ppermute x10, starting transfers between devices, swap(): return lax.ppermute(value, axis, [(0, 1), (1, 0)])  17.1 us
    ppermute x12, starting transfers between devices, shift(): lax.ppermute(value, 'x', [(i, (i + step) % size) for i in range(size)])  15.6 us
    dot_general x14, matrix products, f32_dot(): lax.dot_general(left, right, (dims, ((), ())), preferred_element_type=jnp...  15 us
    all_to_all x2, starting transfers between devices, exchange(): lax.all_to_all(pair, ('y_lo', 'z_hi'), split_axis=0, concat_axis=0, tiled...  13.7 us
  transfers between devices with their start and end apart: 24, of which 15 were waited for; matrix products, arithmetic and copies ran while one was open for 13% of the time, Pallas kernels for 0%

profile of v2, /device:TPU:6, one launch (start us, length us, event | category | flops | bytes accessed | tf_op | source)
XLA Modules:
  0.0 160.3 jit_solution(15953786808809294742)
XLA Ops:
  2.8 1.3 convolution_convert_fusion.4
  5.1 9.6 %all-to-all-start = ((bf16[8,32,1792]{2,1,0:T(8,128)(2,1)}), bf16[8,32,1792]{2,1,0:T(8,128)(2,1)S(1)}, u32[]{:S(2)}, u32[]{:S(2)}) async-start(bf16[8,32,1792]{2,1,0:T(8,128)(2,1)} %pad_maximum_fusion.1), calls=%async_computation | async-start | bytes 1835008 | tf_op jit(solution)/shard_map/all_to_all | solution.py:98
  17.5 20.8 %all-to-all-done = bf16[8,32,1792]{2,1,0:T(8,128)(2,1)S(1)} async-done(((bf16[8,32,1792]{2,1,0:T(8,128)(2,1)}), bf16[8,32,1792]{2,1,0:T(8,128)(2,1)S(1)}, u32[]{:S(2)}, u32[]{:S(2)}) %all-to-all-start) | async-done | bytes 917536 | tf_op jit(solution)/shard_map/all_to_all | solution.py:98
  39.0 1.5 collective-permute-start.2
  40.8 3.9 %collective-permute-start.1 = (bf16[1792,256]{1,0:T(8,128)(2,1)S(1)}, bf16[1792,256]{1,0:T(8,128)(2,1)S(1)}, u32[]{:S(2)}, u32[]{:S(2)}) collective-permute-start(bf16[1792,256]{1,0:T(8,128)(2,1)S(1)} %pad_maximum_fusion.2), channel_id=1, source_target_pairs={{0,4},{4,0},{1,5},{5,1},{2,6},{6,2},{3,7},{7,3},{8,12},{12,8},{9,1... | collective-permute-start | bytes 2752520 | tf_op jit(solution)/shard_map/ppermute | solution.py:36
  45.0 4.2 %collective-permute-done = bf16[128,1792]{1,0:T(8,128)(2,1)S(1)} collective-permute-done((bf16[128,1792]{1,0:T(8,128)(2,1)S(1)}, bf16[128,1792]{1,0:T(8,128)(2,1)S(1)}, u32[]{:S(2)}, u32[]{:S(2)}) %collective-permute-start) | collective-permute-done | bytes 458784 | tf_op jit(solution)/shard_map/ppermute | solution.py:41
  49.2 1.7 %collective-permute-start.11 = (bf16[128,1792]{1,0:T(8,128)(2,1)S(1)}, bf16[128,1792]{1,0:T(8,128)(2,1)S(1)}, u32[]{:S(2)}, u32[]{:S(2)}) collective-permute-start(bf16[128,1792]{1,0:T(8,128)(2,1)S(1)} %bitcast.53), channel_id=1, source_target_pairs={{0,1},{1,2},{2,3},{3,0},{4,5},{5,6},{6,7},{7,4},{8,9},{9,10},{10,1... | collective-permute-start | bytes 1376264 | tf_op jit(solution)/shard_map/ppermute | solution.py:41
  51.2 2.9 %collective-permute-start.3 = (bf16[128,1792]{1,0:T(8,128)(2,1)S(1)}, bf16[128,1792]{1,0:T(8,128)(2,1)S(1)}, u32[]{:S(2)}, u32[]{:S(2)}) collective-permute-start(bf16[128,1792]{1,0:T(8,128)(2,1)S(1)} %collective-permute-done), channel_id=1, source_target_pairs={{0,1},{1,2},{2,3},{3,0},{4,5},{5,6},{6,7},{7,4},{8,9},{9,10},{10,1... | collective-permute-start | bytes 1376264 | tf_op jit(solution)/shard_map/ppermute | solution.py:41
  54.2 11.7 %collective-permute-done.1 = bf16[1792,256]{1,0:T(8,128)(2,1)S(1)} collective-permute-done((bf16[1792,256]{1,0:T(8,128)(2,1)S(1)}, bf16[1792,256]{1,0:T(8,128)(2,1)S(1)}, u32[]{:S(2)}, u32[]{:S(2)}) %collective-permute-start.1) | collective-permute-done | bytes 917536 | tf_op jit(solution)/shard_map/ppermute | solution.py:36
  66.7 2.1 %collective-permute-done.3 = bf16[128,1792]{1,0:T(8,128)(2,1)S(1)} collective-permute-done((bf16[128,1792]{1,0:T(8,128)(2,1)S(1)}, bf16[128,1792]{1,0:T(8,128)(2,1)S(1)}, u32[]{:S(2)}, u32[]{:S(2)}) %collective-permute-start.3) | collective-permute-done | bytes 458784 | tf_op jit(solution)/shard_map/ppermute | solution.py:41
  69.5 3.4 %collective-permute-done.7 = bf16[128,1792]{1,0:T(8,128)(2,1)S(1)} collective-permute-done((bf16[128,1792]{1,0:T(8,128)(2,1)S(1)}, bf16[128,1792]{1,0:T(8,128)(2,1)S(1)}, u32[]{:S(2)}, u32[]{:S(2)}) %collective-permute-start.7) | collective-permute-done | bytes 458784 | tf_op jit(solution)/shard_map/ppermute | solution.py:36
  74.1 3.0 %collective-permute-start.5 = (bf16[256,512]{1,0:T(8,128)(2,1)S(1)}, bf16[256,512]{1,0:T(8,128)(2,1)S(1)}, u32[]{:S(2)}, u32[]{:S(2)}) collective-permute-start(bf16[256,512]{1,0:T(8,128)(2,1)S(1)} %get-tuple-element.36), channel_id=1, source_target_pairs={{0,128},{128,0},{1,129},{129,1},{2,130},{130,2},{3,131},{131,3},{4... | collective-permute-start | bytes 786440 | tf_op jit(solution)/shard_map/ppermute | solution.py:36
  77.2 4.9 %collective-permute-done.5 = bf16[256,512]{1,0:T(8,128)(2,1)S(1)} collective-permute-done((bf16[256,512]{1,0:T(8,128)(2,1)S(1)}, bf16[256,512]{1,0:T(8,128)(2,1)S(1)}, u32[]{:S(2)}, u32[]{:S(2)}) %collective-permute-start.5) | collective-permute-done | bytes 262176 | tf_op jit(solution)/shard_map/ppermute | solution.py:36
  82.4 1.4 collective-permute-done.13
  86.8 3.0 %collective-permute-start.15 = (bf16[256,256]{1,0:T(8,128)(2,1)S(1)}, bf16[256,256]{1,0:T(8,128)(2,1)S(1)}, u32[]{:S(2)}, u32[]{:S(2)}) collective-permute-start(bf16[256,256]{1,0:T(8,128)(2,1)S(1)} %get-tuple-element.34), channel_id=1, source_target_pairs={{0,128},{128,0},{1,129},{129,1},{2,130},{130,2},{3,131},{131,3},{4... | collective-permute-start | bytes 393224 | tf_op jit(solution)/shard_map/ppermute | solution.py:36
  90.3 2.9 %collective-permute-start.8 = (bf16[128,1792]{1,0:T(8,128)(2,1)S(1)}, bf16[128,1792]{1,0:T(8,128)(2,1)S(1)}, u32[]{:S(2)}, u32[]{:S(2)}) collective-permute-start(bf16[128,1792]{1,0:T(8,128)(2,1)S(1)} %get-tuple-element.43), channel_id=1, source_target_pairs={{0,1},{1,2},{2,3},{3,0},{4,5},{5,6},{6,7},{7,4},{8,9},{9,10},{10,1... | collective-permute-start | bytes 1376264 | tf_op jit(solution)/shard_map/ppermute | solution.py:41
  94.3 1.2 convolution_convert_fusion.2
  95.5 4.1 %collective-permute-start.21 = (bf16[128,1792]{1,0:T(8,128)(2,1)}, bf16[128,1792]{1,0:T(8,128)(2,1)}, u32[]{:S(2)}, u32[]{:S(2)}) collective-permute-start(bf16[128,1792]{1,0:T(8,128)(2,1)} %convolution_convert_fusion.2), channel_id=1, source_target_pairs={{0,4},{4,0},{1,5},{5,1},{2,6},{6,2},{3,7},{7,3},{8,12},{12,8},{9,1... | collective-permute-start | bytes 1376264 | tf_op jit(solution)/shard_map/ppermute | solution.py:36
  99.8 1.2 fusion.52
  101.3 1.4 collective-permute-done.8
  102.8 3.8 %collective-permute-start.9 = (bf16[128,1792]{1,0:T(8,128)(2,1)S(1)}, bf16[128,1792]{1,0:T(8,128)(2,1)S(1)}, u32[]{:S(2)}, u32[]{:S(2)}) collective-permute-start(bf16[128,1792]{1,0:T(8,128)(2,1)S(1)} %fusion.11), channel_id=1, source_target_pairs={{0,1},{1,2},{2,3},{3,0},{4,5},{5,6},{6,7},{7,4},{8,9},{9,10},{10,1... | collective-permute-start | bytes 1376264 | tf_op jit(solution)/shard_map/ppermute | solution.py:41
  106.6 1.6 %convolution_convert_fusion = bf16[1792,256]{1,0:T(8,128)(2,1)} fusion(bf16[512,1792]{1,0:T(8,128)(2,1)S(1)} %constant_dynamic-update-slice_fusion.5, bf16[512,512]{1,0:T(8,128)(2,1)S(1)} %maximum_select_fusion), kind=kOutput, calls=%fused_computation.2 | convolution fusion | flops 470220800 | bytes 3014656 | tf_op jit(solution)/shard_map/dot_general | solution.py:32
  108.3 6.7 %collective-permute-done.17 = bf16[128,1792]{1,0:T(8,128)(2,1)S(1)} collective-permute-done((bf16[128,1792]{1,0:T(8,128)(2,1)S(1)}, bf16[128,1792]{1,0:T(8,128)(2,1)S(1)}, u32[]{:S(2)}, u32[]{:S(2)}) %collective-permute-start.17) | collective-permute-done | bytes 458784 | tf_op jit(solution)/shard_map/ppermute | solution.py:41
  114.9 2.4 %collective-permute-start.20 = (bf16[1792,256]{1,0:T(8,128)(2,1)}, bf16[1792,256]{1,0:T(8,128)(2,1)}, u32[]{:S(2)}, u32[]{:S(2)}) collective-permute-start(bf16[1792,256]{1,0:T(8,128)(2,1)} %convolution_convert_fusion), channel_id=1, source_target_pairs={{0,4},{4,0},{1,5},{5,1},{2,6},{6,2},{3,7},{7,3},{8,12},{12,8},{9,1... | collective-permute-start | bytes 2752520 | tf_op jit(solution)/shard_map/ppermute | solution.py:36
  117.7 7.3 %collective-permute-done.19 = bf16[128,1792]{1,0:T(8,128)(2,1)S(1)} collective-permute-done((bf16[128,1792]{1,0:T(8,128)(2,1)S(1)}, bf16[128,1792]{1,0:T(8,128)(2,1)S(1)}, u32[]{:S(2)}, u32[]{:S(2)}) %collective-permute-start.19) | collective-permute-done | bytes 458784 | tf_op jit(solution)/shard_map/ppermute | solution.py:41
  125.0 4.9 %collective-permute-done.18 = bf16[128,1792]{1,0:T(8,128)(2,1)S(1)} collective-permute-done((bf16[128,1792]{1,0:T(8,128)(2,1)S(1)}, bf16[128,1792]{1,0:T(8,128)(2,1)S(1)}, u32[]{:S(2)}, u32[]{:S(2)}) %collective-permute-start.18) | collective-permute-done | bytes 458784 | tf_op jit(solution)/shard_map/ppermute | solution.py:41
  131.0 4.1 %all-to-all-start.1 = ((bf16[8,32,1792]{2,1,0:T(8,128)(2,1)}), bf16[8,32,1792]{2,1,0:T(8,128)(2,1)S(1)}, u32[]{:S(2)}, u32[]{:S(2)}) async-start(bf16[8,32,1792]{2,1,0:T(8,128)(2,1)} %pad_maximum_fusion.4), calls=%async_computation.1 | async-start | bytes 1835008 | tf_op jit(solution)/shard_map/all_to_all | solution.py:98
  135.2 4.2 %fusion.29 = (bf16[128,1792]{1,0:T(8,128)(2,1)}, bf16[128,1792]{1,0:T(8,128)(2,1)}, bf16[128,1792]{1,0:T(8,128)(2,1)}) fusion(bf16[128,1792]{1,0:T(8,128)(2,1)} %param.19, bf16[128,1792]{1,0:T(8,128)(2,1)} %param.18, bf16[128,1792]{1,0:T(8,128)(2,1)} %param.17, bf16[128,1792]{1,0:T(8,128)(2,1)} %collective-permute-done.21, bf16[512,1792]{1,0:T(8,128)(2,1)} %copy-done.7, ...), kind=kOutput, calls=%fused_computation.59 | convolution fusion | flops 239697920 | bytes 5177344 | tf_op jit(solution)/shard_map/dot_general | solution.py:32
  139.4 4.8 %collective-permute-done.20 = bf16[1792,256]{1,0:T(8,128)(2,1)} collective-permute-done((bf16[1792,256]{1,0:T(8,128)(2,1)}, bf16[1792,256]{1,0:T(8,128)(2,1)}, u32[]{:S(2)}, u32[]{:S(2)}) %collective-permute-start.20) | collective-permute-done | bytes 917536 | tf_op jit(solution)/shard_map/ppermute | solution.py:36
  144.2 1.9 %convolution_add_fusion = f32[1792,256]{1,0:T(8,128)S(1)} fusion(bf16[512,1792]{1,0:T(8,128)(2,1)S(1)} %constant_dynamic-update-slice_fusion.5, bf16[1792,256]{1,0:T(8,128)(2,1)} %collective-permute-done.20, bf16[512,512]{1,0:T(8,128)(2,1)S(1)} %copy-done.6), kind=kOutput, calls=%fused_computation | convolution fusion | flops 470679552 | bytes 4849664 | tf_op jit(solution)/shard_map/dot_general | solution.py:32
  147.8 3.1 %fusion.27 = (bf16[2,1792,128]{2,1,0:T(8,128)(2,1)}, bf16[2,1792,128]{2,1,0:T(8,128)(2,1)}, bf16[2,1792,128]{2,1,0:T(8,128)(2,1)}) fusion(f32[1,1792,128]{2,1,0:T(8,128)S(1)} %get-tuple-element.42, f32[1,1792,128]{2,1,0:T(8,128)S(1)} %get-tuple-element.41, bf16[2,1792,128]{2,1,0:T(8,128)(2,1)S(1)} %copy-done.8, bf16[2,1792,128]{2,1,0:T(8,128)(2,1)S(1)} %copy-done.9, ...), kind=kLoop, calls=%fused_computation.54 | loop fusion | flops 9175040 | bytes 7340032 | tf_op jit(solution)/shard_map/convert_element_type | solution.py:27
  150.9 8.0 %all-to-all-done.1 = bf16[8,32,1792]{2,1,0:T(8,128)(2,1)S(1)} async-done(((bf16[8,32,1792]{2,1,0:T(8,128)(2,1)}), bf16[8,32,1792]{2,1,0:T(8,128)(2,1)S(1)}, u32[]{:S(2)}, u32[]{:S(2)}) %all-to-all-start.1) | async-done | bytes 917536 | tf_op jit(solution)/shard_map/all_to_all | solution.py:98
  (104 shorter events, 20.3 us)
Async XLA Ops:
  5.1 11.4 %copy-start.3 = (bf16[2,1792,128]{2,1,0:T(8,128)(2,1)S(1)}, bf16[2,1792,128]{2,1,0:T(8,128)(2,1)}, u32[]{:S(2)}) copy-start(bf16[2,1792,128]{2,1,0:T(8,128)(2,1)} %param.14) | copy-start | bytes 2752516
  5.1 33.2 %all-to-all-start = ((bf16[8,32,1792]{2,1,0:T(8,128)(2,1)}), bf16[8,32,1792]{2,1,0:T(8,128)(2,1)S(1)}, u32[]{:S(2)}, u32[]{:S(2)}) async-start(bf16[8,32,1792]{2,1,0:T(8,128)(2,1)} %pad_maximum_fusion.1), calls=%async_computation | async-start | bytes 1835008 | tf_op jit(solution)/shard_map/all_to_all | solution.py:98
  38.3 2.2 %copy-start.2 = (bf16[1792,128]{1,0:T(8,128)(2,1)S(1)}, bf16[1792,128]{1,0:T(8,128)(2,1)}, u32[]{:S(2)}) copy-start(bf16[1792,128]{1,0:T(8,128)(2,1)} %get-tuple-element.22) | copy-start | bytes 1376260
  38.3 2.3 %copy-start.1 = (bf16[1792,128]{1,0:T(8,128)(2,1)S(1)}, bf16[1792,128]{1,0:T(8,128)(2,1)}, u32[]{:S(2)}) copy-start(bf16[1792,128]{1,0:T(8,128)(2,1)} %get-tuple-element.23) | copy-start | bytes 1376260
  38.4 6.3 %copy-start.11 = (bf16[128,1792]{1,0:T(8,128)(2,1)S(1)}, bf16[128,1792]{1,0:T(8,128)(2,1)}, u32[]{:S(2)}) copy-start(bf16[128,1792]{1,0:T(8,128)(2,1)} %param.17) | copy-start | bytes 1376260
  38.4 10.8 %collective-permute-start = (bf16[128,1792]{1,0:T(8,128)(2,1)S(1)}, bf16[128,1792]{1,0:T(8,128)(2,1)S(1)}, u32[]{:S(2)}, u32[]{:S(2)}) collective-permute-start(bf16[128,1792]{1,0:T(8,128)(2,1)S(1)} %bitcast.57), channel_id=1, source_target_pairs={{0,1},{1,2},{2,3},{3,0},{4,5},{5,6},{6,7},{7,4},{8,9},{9,10},{10,1... | collective-permute-start | bytes 1376264 | tf_op jit(solution)/shard_map/ppermute | solution.py:41
  39.0 11.9 %collective-permute-start.2 = (bf16[128,1792]{1,0:T(8,128)(2,1)S(1)}, bf16[128,1792]{1,0:T(8,128)(2,1)S(1)}, u32[]{:S(2)}, u32[]{:S(2)}) collective-permute-start(bf16[128,1792]{1,0:T(8,128)(2,1)S(1)} %bitcast.58), channel_id=1, source_target_pairs={{0,3},{1,0},{2,1},{3,2},{4,7},{5,4},{6,5},{7,6},{8,11},{9,8},{10,9... | collective-permute-start | bytes 1376264 | tf_op jit(solution)/shard_map/ppermute | solution.py:41
  40.8 25.2 %collective-permute-start.1 = (bf16[1792,256]{1,0:T(8,128)(2,1)S(1)}, bf16[1792,256]{1,0:T(8,128)(2,1)S(1)}, u32[]{:S(2)}, u32[]{:S(2)}) collective-permute-start(bf16[1792,256]{1,0:T(8,128)(2,1)S(1)} %pad_maximum_fusion.2), channel_id=1, source_target_pairs={{0,4},{4,0},{1,5},{5,1},{2,6},{6,2},{3,7},{7,3},{8,12},{12,8},{9,1... | collective-permute-start | bytes 2752520 | tf_op jit(solution)/shard_map/ppermute | solution.py:36
  44.7 28.2 %collective-permute-start.7 = (bf16[128,1792]{1,0:T(8,128)(2,1)S(1)}, bf16[128,1792]{1,0:T(8,128)(2,1)S(1)}, u32[]{:S(2)}, u32[]{:S(2)}) collective-permute-start(bf16[128,1792]{1,0:T(8,128)(2,1)S(1)} %copy-done.11), channel_id=1, source_target_pairs={{0,4},{4,0},{1,5},{5,1},{2,6},{6,2},{3,7},{7,3},{8,12},{12,8},{9,1... | collective-permute-start | bytes 1376264 | tf_op jit(solution)/shard_map/ppermute | solution.py:36
  49.2 24.7 %collective-permute-start.11 = (bf16[128,1792]{1,0:T(8,128)(2,1)S(1)}, bf16[128,1792]{1,0:T(8,128)(2,1)S(1)}, u32[]{:S(2)}, u32[]{:S(2)}) collective-permute-start(bf16[128,1792]{1,0:T(8,128)(2,1)S(1)} %bitcast.53), channel_id=1, source_target_pairs={{0,1},{1,2},{2,3},{3,0},{4,5},{5,6},{6,7},{7,4},{8,9},{9,10},{10,1... | collective-permute-start | bytes 1376264 | tf_op jit(solution)/shard_map/ppermute | solution.py:41
  50.9 22.0 %collective-permute-start.12 = (bf16[128,1792]{1,0:T(8,128)(2,1)S(1)}, bf16[128,1792]{1,0:T(8,128)(2,1)S(1)}, u32[]{:S(2)}, u32[]{:S(2)}) collective-permute-start(bf16[128,1792]{1,0:T(8,128)(2,1)S(1)} %bitcast.54), channel_id=1, source_target_pairs={{0,3},{1,0},{2,1},{3,2},{4,7},{5,4},{6,5},{7,6},{8,11},{9,8},{10,9... | collective-permute-start | bytes 1376264 | tf_op jit(solution)/shard_map/ppermute | solution.py:41
  51.2 17.6 %collective-permute-start.3 = (bf16[128,1792]{1,0:T(8,128)(2,1)S(1)}, bf16[128,1792]{1,0:T(8,128)(2,1)S(1)}, u32[]{:S(2)}, u32[]{:S(2)}) collective-permute-start(bf16[128,1792]{1,0:T(8,128)(2,1)S(1)} %collective-permute-done), channel_id=1, source_target_pairs={{0,1},{1,2},{2,3},{3,0},{4,5},{5,6},{6,7},{7,4},{8,9},{9,10},{10,1... | collective-permute-start | bytes 1376264 | tf_op jit(solution)/shard_map/ppermute | solution.py:41
  69.4 4.5 %collective-permute-start.4 = (f32[256,512]{1,0:T(8,128)S(1)}, f32[256,512]{1,0:T(8,128)S(1)}, u32[]{:S(2)}, u32[]{:S(2)}) collective-permute-start(f32[256,512]{1,0:T(8,128)S(1)} %get-tuple-element.69), channel_id=1, source_target_pairs={{0,64},{64,0},{1,65},{65,1},{2,66},{66,2},{3,67},{67,3},{4,68},{68... | collective-permute-start | bytes 1572872 | tf_op jit(solution)/shard_map/ppermute | solution.py:36
  72.9 10.9 %collective-permute-start.13 = (bf16[128,1792]{1,0:T(8,128)(2,1)S(1)}, bf16[128,1792]{1,0:T(8,128)(2,1)S(1)}, u32[]{:S(2)}, u32[]{:S(2)}) collective-permute-start(bf16[128,1792]{1,0:T(8,128)(2,1)S(1)} %collective-permute-done.12), channel_id=1, source_target_pairs={{0,3},{1,0},{2,1},{3,2},{4,7},{5,4},{6,5},{7,6},{8,11},{9,8},{10,9... | collective-permute-start | bytes 1376264 | tf_op jit(solution)/shard_map/ppermute | solution.py:41
  74.1 8.0 %collective-permute-start.5 = (bf16[256,512]{1,0:T(8,128)(2,1)S(1)}, bf16[256,512]{1,0:T(8,128)(2,1)S(1)}, u32[]{:S(2)}, u32[]{:S(2)}) collective-permute-start(bf16[256,512]{1,0:T(8,128)(2,1)S(1)} %get-tuple-element.36), channel_id=1, source_target_pairs={{0,128},{128,0},{1,129},{129,1},{2,130},{130,2},{3,131},{131,3},{4... | collective-permute-start | bytes 786440 | tf_op jit(solution)/shard_map/ppermute | solution.py:36
  82.3 1.5 collective-permute-start.6
  83.9 10.4 %copy-start.7 = (bf16[512,1792]{1,0:T(8,128)(2,1)}, bf16[512,1792]{1,0:T(8,128)(2,1)S(1)}, u32[]{:S(2)}) copy-start(bf16[512,1792]{1,0:T(8,128)(2,1)S(1)} %constant_dynamic-update-slice_fusion.9) | copy-start | bytes 5505028
  84.9 1.8 %collective-permute-start.14 = (f32[256,256]{1,0:T(8,128)S(1)}, f32[256,256]{1,0:T(8,128)S(1)}, u32[]{:S(2)}, u32[]{:S(2)}) collective-permute-start(f32[256,256]{1,0:T(8,128)S(1)} %get-tuple-element.71), channel_id=1, source_target_pairs={{0,64},{64,0},{1,65},{65,1},{2,66},{66,2},{3,67},{67,3},{4,68},{68... | collective-permute-start | bytes 786440 | tf_op jit(solution)/shard_map/ppermute | solution.py:36
  86.8 7.1 %collective-permute-start.15 = (bf16[256,256]{1,0:T(8,128)(2,1)S(1)}, bf16[256,256]{1,0:T(8,128)(2,1)S(1)}, u32[]{:S(2)}, u32[]{:S(2)}) collective-permute-start(bf16[256,256]{1,0:T(8,128)(2,1)S(1)} %get-tuple-element.34), channel_id=1, source_target_pairs={{0,128},{128,0},{1,129},{129,1},{2,130},{130,2},{3,131},{131,3},{4... | collective-permute-start | bytes 393224 | tf_op jit(solution)/shard_map/ppermute | solution.py:36
  89.9 27.5 %collective-permute-start.10 = (bf16[128,1792]{1,0:T(8,128)(2,1)S(1)}, bf16[128,1792]{1,0:T(8,128)(2,1)S(1)}, u32[]{:S(2)}, u32[]{:S(2)}) collective-permute-start(bf16[128,1792]{1,0:T(8,128)(2,1)S(1)} %get-tuple-element.44), channel_id=1, source_target_pairs={{0,3},{1,0},{2,1},{3,2},{4,7},{5,4},{6,5},{7,6},{8,11},{9,8},{10,9... | collective-permute-start | bytes 1376264 | tf_op jit(solution)/shard_map/ppermute | solution.py:41
  90.3 12.4 %collective-permute-start.8 = (bf16[128,1792]{1,0:T(8,128)(2,1)S(1)}, bf16[128,1792]{1,0:T(8,128)(2,1)S(1)}, u32[]{:S(2)}, u32[]{:S(2)}) collective-permute-start(bf16[128,1792]{1,0:T(8,128)(2,1)S(1)} %get-tuple-element.43), channel_id=1, source_target_pairs={{0,1},{1,2},{2,3},{3,0},{4,5},{5,6},{6,7},{7,4},{8,9},{9,10},{10,1... | collective-permute-start | bytes 1376264 | tf_op jit(solution)/shard_map/ppermute | solution.py:41
  94.2 5.4 %collective-permute-start.16 = (bf16[256,512]{1,0:T(8,128)(2,1)S(1)}, bf16[256,512]{1,0:T(8,128)(2,1)S(1)}, u32[]{:S(2)}, u32[]{:S(2)}) collective-permute-start(bf16[256,512]{1,0:T(8,128)(2,1)S(1)} %pad_maximum_fusion.7), channel_id=1, source_target_pairs={{0,64},{64,0},{1,65},{65,1},{2,66},{66,2},{3,67},{67,3},{4,68},{68... | collective-permute-start | bytes 786440 | tf_op jit(solution)/shard_map/ppermute | solution.py:36
  95.5 39.6 %collective-permute-start.21 = (bf16[128,1792]{1,0:T(8,128)(2,1)}, bf16[128,1792]{1,0:T(8,128)(2,1)}, u32[]{:S(2)}, u32[]{:S(2)}) collective-permute-start(bf16[128,1792]{1,0:T(8,128)(2,1)} %convolution_convert_fusion.2), channel_id=1, source_target_pairs={{0,4},{4,0},{1,5},{5,1},{2,6},{6,2},{3,7},{7,3},{8,12},{12,8},{9,1... | collective-permute-start | bytes 1376264 | tf_op jit(solution)/shard_map/ppermute | solution.py:36
  99.8 6.9 %copy-start.5 = (bf16[512,512]{1,0:T(8,128)(2,1)}, bf16[512,512]{1,0:T(8,128)(2,1)S(1)}, u32[]{:S(2)}) copy-start(bf16[512,512]{1,0:T(8,128)(2,1)S(1)} %maximum_select_fusion) | copy-start | bytes 1572868
  101.0 13.9 %collective-permute-start.17 = (bf16[128,1792]{1,0:T(8,128)(2,1)S(1)}, bf16[128,1792]{1,0:T(8,128)(2,1)S(1)}, u32[]{:S(2)}, u32[]{:S(2)}) collective-permute-start(bf16[128,1792]{1,0:T(8,128)(2,1)S(1)} %get-tuple-element.45), channel_id=1, source_target_pairs={{0,3},{1,0},{2,1},{3,2},{4,7},{5,4},{6,5},{7,6},{8,11},{9,8},{10,9... | collective-permute-start | bytes 1376264 | tf_op jit(solution)/shard_map/ppermute | solution.py:41
  102.8 14.7 %collective-permute-start.9 = (bf16[128,1792]{1,0:T(8,128)(2,1)S(1)}, bf16[128,1792]{1,0:T(8,128)(2,1)S(1)}, u32[]{:S(2)}, u32[]{:S(2)}) collective-permute-start(bf16[128,1792]{1,0:T(8,128)(2,1)S(1)} %fusion.11), channel_id=1, source_target_pairs={{0,1},{1,2},{2,3},{3,0},{4,5},{5,6},{6,7},{7,4},{8,9},{9,10},{10,1... | collective-permute-start | bytes 1376264 | tf_op jit(solution)/shard_map/ppermute | solution.py:41
  106.5 18.4 %collective-permute-start.19 = (bf16[128,1792]{1,0:T(8,128)(2,1)S(1)}, bf16[128,1792]{1,0:T(8,128)(2,1)S(1)}, u32[]{:S(2)}, u32[]{:S(2)}) collective-permute-start(bf16[128,1792]{1,0:T(8,128)(2,1)S(1)} %get-tuple-element.46), channel_id=1, source_target_pairs={{0,1},{1,2},{2,3},{3,0},{4,5},{5,6},{6,7},{7,4},{8,9},{9,10},{10,1... | collective-permute-start | bytes 1376264 | tf_op jit(solution)/shard_map/ppermute | solution.py:41
  114.9 29.2 %collective-permute-start.20 = (bf16[1792,256]{1,0:T(8,128)(2,1)}, bf16[1792,256]{1,0:T(8,128)(2,1)}, u32[]{:S(2)}, u32[]{:S(2)}) collective-permute-start(bf16[1792,256]{1,0:T(8,128)(2,1)} %convolution_convert_fusion), channel_id=1, source_target_pairs={{0,4},{4,0},{1,5},{5,1},{2,6},{6,2},{3,7},{7,3},{8,12},{12,8},{9,1... | collective-permute-start | bytes 2752520 | tf_op jit(solution)/shard_map/ppermute | solution.py:36
  117.4 12.4 %collective-permute-start.18 = (bf16[128,1792]{1,0:T(8,128)(2,1)S(1)}, bf16[128,1792]{1,0:T(8,128)(2,1)S(1)}, u32[]{:S(2)}, u32[]{:S(2)}) collective-permute-start(bf16[128,1792]{1,0:T(8,128)(2,1)S(1)} %fusion.8), channel_id=1, source_target_pairs={{0,3},{1,0},{2,1},{3,2},{4,7},{5,4},{6,5},{7,6},{8,11},{9,8},{10,9... | collective-permute-start | bytes 1376264 | tf_op jit(solution)/shard_map/ppermute | solution.py:41
  131.0 27.8 %all-to-all-start.1 = ((bf16[8,32,1792]{2,1,0:T(8,128)(2,1)}), bf16[8,32,1792]{2,1,0:T(8,128)(2,1)S(1)}, u32[]{:S(2)}, u32[]{:S(2)}) async-start(bf16[8,32,1792]{2,1,0:T(8,128)(2,1)} %pad_maximum_fusion.4), calls=%async_computation.1 | async-start | bytes 1835008 | tf_op jit(solution)/shard_map/all_to_all | solution.py:98
  135.1 9.0 %copy-start.6 = (bf16[512,512]{1,0:T(8,128)(2,1)S(1)}, bf16[512,512]{1,0:T(8,128)(2,1)}, u32[]{:S(2)}) copy-start(bf16[512,512]{1,0:T(8,128)(2,1)} %copy-done.5) | copy-start | bytes 1572868
  147.8 11.1 %copy-start.10 = (bf16[8,32,256]{2,1,0:T(8,128)(2,1)S(1)}, bf16[8,32,256]{2,1,0:T(8,128)(2,1)}, u32[]{:S(2)}) copy-start(bf16[8,32,256]{2,1,0:T(8,128)(2,1)} %fusion.33) | copy-start | bytes 393220
  (4 other events, 6.2 us)

commit v3 on v2

--- a/solution.py
+++ b/solution.py
@@ -1,6 +1,7 @@
 import jax
 import jax.numpy as jnp
 from jax import lax
+from jax.experimental import pallas as pl
 from jax.sharding import Mesh
 from jax.sharding import PartitionSpec as P
 
@@ -47,6 +48,45 @@
 
 def to_bf16(value):
     return value.astype(jnp.bfloat16)
+
+
+EXPERTS = 8
+CAPACITY = 16
+
+
+def dispatch_kernel(index_ref, gates_ref, tokens_ref, grads_ref, send_ref, combine_ref):
+    index = index_ref[...]
+    gates = gates_ref[...].astype(jnp.float32)
+    count = index.shape[1]
+    hits = [index == e for e in range(EXPERTS)]
+    members = [jnp.sum(jnp.where(hit, 1.0, 0.0), axis=0, keepdims=True) for hit in hits]
+    gate_rows = [jnp.sum(jnp.where(hit, gates, 0.0), axis=0, keepdims=True) for hit in hits]
+    member = jnp.concatenate(members, axis=0)
+    earlier = lax.broadcasted_iota(jnp.int32, (count, count), 0) < lax.broadcasted_iota(
+        jnp.int32, (count, count), 1
+    )
+    slot = f32_dot(
+        member.astype(jnp.bfloat16),
+        jnp.where(earlier, 1.0, 0.0).astype(jnp.bfloat16),
+        ((1,), (0,)),
+    )
+    slots = lax.broadcasted_iota(jnp.int32, (CAPACITY, count), 0).astype(jnp.float32)
+    select, weigh = [], []
+    for e in range(EXPERTS):
+        here = (slots == slot[e : e + 1]) & (member[e : e + 1] > 0.5)
+        select.append(jnp.where(here, 1.0, 0.0))
+        weigh.append(jnp.where(here, gate_rows[e], 0.0))
+    select = jnp.concatenate(select, axis=0).astype(jnp.bfloat16)
+    weigh = jnp.concatenate(weigh, axis=0).astype(jnp.bfloat16)
+    token_rows = f32_dot(select, tokens_ref[...], ((1,), (0,))).astype(jnp.bfloat16)
+    grad_rows = f32_dot(weigh, grads_ref[...], ((1,), (0,))).astype(jnp.bfloat16)
+    combine_ref[...] = jnp.zeros(combine_ref.shape, jnp.bfloat16)
+    for e in range(EXPERTS):
+        rows = slice(e * CAPACITY, (e + 1) * CAPACITY)
+        send_ref[e, :CAPACITY, :] = token_rows[rows]
+        send_ref[e, CAPACITY:, :] = grad_rows[rows]
+        combine_ref[e, :CAPACITY, :count] = weigh[rows]
+        combine_ref[e, CAPACITY:, count:] = select[rows]
 
 
 def per_device(
@@ -61,41 +101,32 @@
     down_m,
     down_v,
 ):
-    expert_list = lax.axis_size("y_lo") * lax.axis_size("z_hi")
+    expert_list = EXPERTS
     tok_dev, width_dev = tokens.shape
     hidden = gate_up.shape[2]
-    capacity = 16
+    capacity = CAPACITY
     rows = expert_list * capacity
 
-    experts = jnp.arange(expert_list, dtype=jnp.int32)[:, None, None]
-    index_t = routed_expert_index.T
-    gates_t = route_gates.T.astype(jnp.float32)
-    named = (index_t[None] == experts).astype(jnp.float32)
-    member = jnp.sum(named, axis=1)
-    gate_of = jnp.sum(named * gates_t[None], axis=1)
-    earlier = (
-        lax.broadcasted_iota(jnp.int32, (tok_dev, tok_dev), 0)
-        < lax.broadcasted_iota(jnp.int32, (tok_dev, tok_dev), 1)
-    ).astype(jnp.bfloat16)
-    slot = f32_dot(to_bf16(member), earlier, ((1,), (0,))).astype(jnp.int32)
-    slots = lax.broadcasted_iota(jnp.int32, (expert_list, capacity, tok_dev), 1)
-    here = (slots == slot[:, None, :]) & (member[:, None, :] > 0.5)
-    selector = here.astype(jnp.bfloat16).reshape(rows, tok_dev)
-    gate_selector = to_bf16(jnp.where(here, gate_of[:, None, :], 0.0)).reshape(rows, tok_dev)
+    send, combine = pl.pallas_call(
+        dispatch_kernel,
+        out_shape=(
+            jax.ShapeDtypeStruct((expert_list, 2 * capacity, width_dev), jnp.bfloat16),
+            jax.ShapeDtypeStruct((expert_list, 2 * capacity, 2 * tok_dev), jnp.bfloat16),
+        ),
+        name="dispatch",
+    )(routed_expert_index.T, route_gates.T, tokens, grad_out)
+    combine = combine.reshape(2 * rows, 2 * tok_dev)
 
     core = lax.axis_index("core")
     y_hi = lax.axis_index("y_hi")
     mid = rows // 2
 
-    def exchange(first, second):
-        pair = jnp.concatenate(
-            (
-                first.reshape(expert_list, capacity, width_dev),
-                second.reshape(expert_list, capacity, width_dev),
-            ),
-            axis=1,
-        )
+    def exchange(pair):
         return lax.all_to_all(pair, ("y_lo", "z_hi"), split_axis=0, concat_axis=0, tiled=True)
+
+    def interleave(first, second):
+        shape = (expert_list, capacity, width_dev)
+        return jnp.concatenate((first.reshape(shape), second.reshape(shape)), axis=1)
 
     def core_sum(low, high):
         keep = jnp.where(core == 0, low, high)
@@ -118,20 +149,7 @@
             axis=1,
         )
 
-    nothing = jnp.zeros_like(here, dtype=jnp.bfloat16)
-    sel3 = here.astype(jnp.bfloat16)
-    gate3 = gate_selector.reshape(sel3.shape)
-    combine = jnp.concatenate(
-        (
-            jnp.concatenate((gate3, nothing), axis=2),
-            jnp.concatenate((nothing, sel3), axis=2),
-        ),
-        axis=1,
-    ).reshape(2 * rows, 2 * tok_dev)
-
-    tok_rows = to_bf16(f32_dot(selector, tokens, ((1,), (0,))))
-    grad_rows = to_bf16(f32_dot(gate_selector, grad_out, ((1,), (0,))))
-    got = exchange(tok_rows, grad_rows)
+    got = exchange(send)
     tok_own = got[:, :capacity].reshape(rows, width_dev)
     grad_own = got[:, capacity:].reshape(rows, width_dev)
     tok_own, grad_own, gate, up, down_late, combine = lax.optimization_barrier(
@@ -192,7 +210,7 @@
         )
     )
     delta_sum = scatter_x(f32_dot(d_paired, paired, ((1,), (1,))), -1)
-    returned = exchange(mixed_sum, delta_sum)
+    returned = exchange(interleave(mixed_sum, delta_sum))
 
     grad_down_far = to_bf16(f32_dot(scaled[:, hidden:], grad_all, ((0,), (0,))))
     grad_down_in = swap(grad_down_far, "z_lo")

time: 161 us -> 159 us (0.988)
  other arithmetic: 9.03 us -> 5.64 us
  Pallas kernels: 0 us -> 2.75 us
  waiting for transfers between devices: 83.1 us -> 85.7 us
  matrix products: 15 us -> 13.2 us
    pallas_call x0 -> x1, Pallas kernels: none -> 2.75 us  [per_device(): pl.pallas_call(dispatch_kernel, out_shape=(jax.ShapeDtypeStruct((expert_l...]
    all_to_all x2, waiting for transfers between devices: 28.8 us -> 30.8 us  [exchange(): lax.all_to_all(pair, ('y_lo', 'z_hi'), split_axis=0, concat_axis=0, tiled...]
    dot_general x14 -> x11, matrix products: 15 us -> 13.2 us  [f32_dot(): lax.dot_general(left, right, (dims, ((), ())), preferred_element_type=jnp...]
    concatenate x4 -> x1, other arithmetic: 2.7 us -> 1.02 us  [interleave(): jnp.concatenate((first.reshape(shape), second.reshape(shape)), axis=1)]
  transfers between devices with their start and end apart: 24 -> 24, of which waited for: 15 -> 16; matrix products, arithmetic and copies ran while one was open for 13% -> 12% of each run, Pallas kernels for 0% -> 0%
where the time goes in v3:
time: 159 us; the launch traced here: 158 us
  waiting for transfers between devices  85.7 us (54%)
  starting transfers between devices  45.7 us (29%)
  matrix products  13.2 us (8%)
  other arithmetic  5.64 us (4%)
  local copies, waits for them, and re-layouts  4.38 us (3%)
  Pallas kernels  2.75 us (2%)
    all_to_all x2, waiting for transfers between devices, exchange(): lax.all_to_all(pair, ('y_lo', 'z_hi'), split_axis=0, concat_axis=0, tiled...  30.8 us
    ppermute x12, waiting for transfers between devices, shift(): lax.ppermute(value, 'x', [(i, (i + step) % size) for i in range(size)])  28.5 us
    ppermute x10, waiting for transfers between devices, swap(): return lax.ppermute(value, axis, [(0, 1), (1, 0)])  26.4 us
    ppermute x10, starting transfers between devices, swap(): return lax.ppermute(value, axis, [(0, 1), (1, 0)])  17.1 us
    ppermute x12, starting transfers between devices, shift(): lax.ppermute(value, 'x', [(i, (i + step) % size) for i in range(size)])  15 us
    all_to_all x2, starting transfers between devices, exchange(): lax.all_to_all(pair, ('y_lo', 'z_hi'), split_axis=0, concat_axis=0, tiled...  13.6 us
    dot_general x11, matrix products, f32_dot(): lax.dot_general(left, right, (dims, ((), ())), preferred_element_type=jnp...  13.2 us
  transfers between devices with their start and end apart: 24, of which 16 were waited for; matrix products, arithmetic and copies ran while one was open for 12% of the time, Pallas kernels for 0%

profile of v3, /device:TPU:6, one launch (start us, length us, event | category | flops | bytes accessed | tf_op | source)
XLA Modules:
  0.0 158.5 jit_solution(18120478991341603646)
XLA Ops:
  0.7 2.7 %dispatch.1 = (bf16[8,32,1792]{2,1,0:T(8,128)(2,1)}, bf16[8,32,256]{2,1,0:T(8,128)(2,1)}) custom-call(s32[8,128]{1,0:T(8,128)} %bitcast.43, bf16[8,128]{1,0:T(8,128)(2,1)} %bitcast.44, bf16[128,1792]{1,0:T(8,128)(2,1)} %tokens_ref.1, bf16[128,1792]{1,0:T(8,128)(2,1)} %grads_ref.1), custom_call_target="tpu_custom_call" | custom-call | tf_op jit(solution)/shard_map/dispatch/pallas_call | solution.py:110
  3.4 9.5 %all-to-all-start = ((bf16[8,32,1792]{2,1,0:T(8,128)(2,1)}), bf16[8,32,1792]{2,1,0:T(8,128)(2,1)S(1)}, u32[]{:S(2)}, u32[]{:S(2)}) async-start(bf16[8,32,1792]{2,1,0:T(8,128)(2,1)} %get-tuple-element.22), calls=%async_computation | async-start | bytes 1835008 | tf_op jit(solution)/shard_map/all_to_all | solution.py:125
  13.8 22.8 %all-to-all-done = bf16[8,32,1792]{2,1,0:T(8,128)(2,1)S(1)} async-done(((bf16[8,32,1792]{2,1,0:T(8,128)(2,1)}), bf16[8,32,1792]{2,1,0:T(8,128)(2,1)S(1)}, u32[]{:S(2)}, u32[]{:S(2)}) %all-to-all-start) | async-done | bytes 917536 | tf_op jit(solution)/shard_map/all_to_all | solution.py:125
  36.9 1.8 %collective-permute-start.2 = (bf16[128,1792]{1,0:T(8,128)(2,1)S(1)}, bf16[128,1792]{1,0:T(8,128)(2,1)S(1)}, u32[]{:S(2)}, u32[]{:S(2)}) collective-permute-start(bf16[128,1792]{1,0:T(8,128)(2,1)S(1)} %bitcast.37), channel_id=1, source_target_pairs={{0,3},{1,0},{2,1},{3,2},{4,7},{5,4},{6,5},{7,6},{8,11},{9,8},{10,9... | collective-permute-start | bytes 1376264 | tf_op jit(solution)/shard_map/ppermute | solution.py:42
  39.0 3.9 %collective-permute-start.1 = (bf16[1792,256]{1,0:T(8,128)(2,1)S(1)}, bf16[1792,256]{1,0:T(8,128)(2,1)S(1)}, u32[]{:S(2)}, u32[]{:S(2)}) collective-permute-start(bf16[1792,256]{1,0:T(8,128)(2,1)S(1)} %pad_maximum_fusion.1), channel_id=1, source_target_pairs={{0,4},{4,0},{1,5},{5,1},{2,6},{6,2},{3,7},{7,3},{8,12},{12,8},{9,1... | collective-permute-start | bytes 2752520 | tf_op jit(solution)/shard_map/ppermute | solution.py:37
  43.1 4.3 %collective-permute-done = bf16[128,1792]{1,0:T(8,128)(2,1)S(1)} collective-permute-done((bf16[128,1792]{1,0:T(8,128)(2,1)S(1)}, bf16[128,1792]{1,0:T(8,128)(2,1)S(1)}, u32[]{:S(2)}, u32[]{:S(2)}) %collective-permute-start) | collective-permute-done | bytes 458784 | tf_op jit(solution)/shard_map/ppermute | solution.py:42
  47.4 1.5 collective-permute-start.11
  49.4 2.7 %collective-permute-start.3 = (bf16[128,1792]{1,0:T(8,128)(2,1)S(1)}, bf16[128,1792]{1,0:T(8,128)(2,1)S(1)}, u32[]{:S(2)}, u32[]{:S(2)}) collective-permute-start(bf16[128,1792]{1,0:T(8,128)(2,1)S(1)} %collective-permute-done), channel_id=1, source_target_pairs={{0,1},{1,2},{2,3},{3,0},{4,5},{5,6},{6,7},{7,4},{8,9},{9,10},{10,1... | collective-permute-start | bytes 1376264 | tf_op jit(solution)/shard_map/ppermute | solution.py:42
  52.2 11.9 %collective-permute-done.1 = bf16[1792,256]{1,0:T(8,128)(2,1)S(1)} collective-permute-done((bf16[1792,256]{1,0:T(8,128)(2,1)S(1)}, bf16[1792,256]{1,0:T(8,128)(2,1)S(1)}, u32[]{:S(2)}, u32[]{:S(2)}) %collective-permute-start.1) | collective-permute-done | bytes 917536 | tf_op jit(solution)/shard_map/ppermute | solution.py:37
  64.8 2.2 %collective-permute-done.3 = bf16[128,1792]{1,0:T(8,128)(2,1)S(1)} collective-permute-done((bf16[128,1792]{1,0:T(8,128)(2,1)S(1)}, bf16[128,1792]{1,0:T(8,128)(2,1)S(1)}, u32[]{:S(2)}, u32[]{:S(2)}) %collective-permute-start.3) | collective-permute-done | bytes 458784 | tf_op jit(solution)/shard_map/ppermute | solution.py:42
  67.8 3.3 %collective-permute-done.7 = bf16[128,1792]{1,0:T(8,128)(2,1)S(1)} collective-permute-done((bf16[128,1792]{1,0:T(8,128)(2,1)S(1)}, bf16[128,1792]{1,0:T(8,128)(2,1)S(1)}, u32[]{:S(2)}, u32[]{:S(2)}) %collective-permute-start.7) | collective-permute-done | bytes 458784 | tf_op jit(solution)/shard_map/ppermute | solution.py:37
  72.2 3.1 %collective-permute-start.5 = (bf16[256,512]{1,0:T(8,128)(2,1)S(1)}, bf16[256,512]{1,0:T(8,128)(2,1)S(1)}, u32[]{:S(2)}, u32[]{:S(2)}) collective-permute-start(bf16[256,512]{1,0:T(8,128)(2,1)S(1)} %get-tuple-element.38), channel_id=1, source_target_pairs={{0,128},{128,0},{1,129},{129,1},{2,130},{130,2},{3,131},{131,3},{4... | collective-permute-start | bytes 786440 | tf_op jit(solution)/shard_map/ppermute | solution.py:37
  75.4 4.8 %collective-permute-done.5 = bf16[256,512]{1,0:T(8,128)(2,1)S(1)} collective-permute-done((bf16[256,512]{1,0:T(8,128)(2,1)S(1)}, bf16[256,512]{1,0:T(8,128)(2,1)S(1)}, u32[]{:S(2)}, u32[]{:S(2)}) %collective-permute-start.5) | collective-permute-done | bytes 262176 | tf_op jit(solution)/shard_map/ppermute | solution.py:37
  80.5 1.5 collective-permute-done.13
  84.8 3.3 %collective-permute-start.15 = (bf16[256,256]{1,0:T(8,128)(2,1)S(1)}, bf16[256,256]{1,0:T(8,128)(2,1)S(1)}, u32[]{:S(2)}, u32[]{:S(2)}) collective-permute-start(bf16[256,256]{1,0:T(8,128)(2,1)S(1)} %get-tuple-element.36), channel_id=1, source_target_pairs={{0,128},{128,0},{1,129},{129,1},{2,130},{130,2},{3,131},{131,3},{4... | collective-permute-start | bytes 393224 | tf_op jit(solution)/shard_map/ppermute | solution.py:37
  88.5 2.9 %collective-permute-start.8 = (bf16[128,1792]{1,0:T(8,128)(2,1)S(1)}, bf16[128,1792]{1,0:T(8,128)(2,1)S(1)}, u32[]{:S(2)}, u32[]{:S(2)}) collective-permute-start(bf16[128,1792]{1,0:T(8,128)(2,1)S(1)} %get-tuple-element.45), channel_id=1, source_target_pairs={{0,1},{1,2},{2,3},{3,0},{4,5},{5,6},{6,7},{7,4},{8,9},{9,10},{10,1... | collective-permute-start | bytes 1376264 | tf_op jit(solution)/shard_map/ppermute | solution.py:42
  92.5 1.2 convolution_convert_fusion.2
  93.7 4.1 %collective-permute-start.21 = (bf16[128,1792]{1,0:T(8,128)(2,1)}, bf16[128,1792]{1,0:T(8,128)(2,1)}, u32[]{:S(2)}, u32[]{:S(2)}) collective-permute-start(bf16[128,1792]{1,0:T(8,128)(2,1)} %convolution_convert_fusion.2), channel_id=1, source_target_pairs={{0,4},{4,0},{1,5},{5,1},{2,6},{6,2},{3,7},{7,3},{8,12},{12,8},{9,1... | collective-permute-start | bytes 1376264 | tf_op jit(solution)/shard_map/ppermute | solution.py:37
  98.0 1.1 fusion.46
  99.3 1.6 %collective-permute-done.8 = bf16[128,1792]{1,0:T(8,128)(2,1)S(1)} collective-permute-done((bf16[128,1792]{1,0:T(8,128)(2,1)S(1)}, bf16[128,1792]{1,0:T(8,128)(2,1)S(1)}, u32[]{:S(2)}, u32[]{:S(2)}) %collective-permute-start.8) | collective-permute-done | bytes 458784 | tf_op jit(solution)/shard_map/ppermute | solution.py:42
  101.0 3.8 %collective-permute-start.9 = (bf16[128,1792]{1,0:T(8,128)(2,1)S(1)}, bf16[128,1792]{1,0:T(8,128)(2,1)S(1)}, u32[]{:S(2)}, u32[]{:S(2)}) collective-permute-start(bf16[128,1792]{1,0:T(8,128)(2,1)S(1)} %fusion.11), channel_id=1, source_target_pairs={{0,1},{1,2},{2,3},{3,0},{4,5},{5,6},{6,7},{7,4},{8,9},{9,10},{10,1... | collective-permute-start | bytes 1376264 | tf_op jit(solution)/shard_map/ppermute | solution.py:42
  104.9 1.6 %convolution_convert_fusion = bf16[1792,256]{1,0:T(8,128)(2,1)} fusion(bf16[512,1792]{1,0:T(8,128)(2,1)S(1)} %constant_dynamic-update-slice_fusion.5, bf16[512,512]{1,0:T(8,128)(2,1)S(1)} %maximum_select_fusion), kind=kOutput, calls=%fused_computation.2 | convolution fusion | flops 470220800 | bytes 3014656 | tf_op jit(solution)/shard_map/dot_general | solution.py:33
  106.5 6.7 %collective-permute-done.17 = bf16[128,1792]{1,0:T(8,128)(2,1)S(1)} collective-permute-done((bf16[128,1792]{1,0:T(8,128)(2,1)S(1)}, bf16[128,1792]{1,0:T(8,128)(2,1)S(1)}, u32[]{:S(2)}, u32[]{:S(2)}) %collective-permute-start.17) | collective-permute-done | bytes 458784 | tf_op jit(solution)/shard_map/ppermute | solution.py:42
  113.1 2.3 %collective-permute-start.20 = (bf16[1792,256]{1,0:T(8,128)(2,1)}, bf16[1792,256]{1,0:T(8,128)(2,1)}, u32[]{:S(2)}, u32[]{:S(2)}) collective-permute-start(bf16[1792,256]{1,0:T(8,128)(2,1)} %convolution_convert_fusion), channel_id=1, source_target_pairs={{0,4},{4,0},{1,5},{5,1},{2,6},{6,2},{3,7},{7,3},{8,12},{12,8},{9,1... | collective-permute-start | bytes 2752520 | tf_op jit(solution)/shard_map/ppermute | solution.py:37
  115.9 7.3 %collective-permute-done.19 = bf16[128,1792]{1,0:T(8,128)(2,1)S(1)} collective-permute-done((bf16[128,1792]{1,0:T(8,128)(2,1)S(1)}, bf16[128,1792]{1,0:T(8,128)(2,1)S(1)}, u32[]{:S(2)}, u32[]{:S(2)}) %collective-permute-start.19) | collective-permute-done | bytes 458784 | tf_op jit(solution)/shard_map/ppermute | solution.py:42
  123.2 4.7 %collective-permute-done.18 = bf16[128,1792]{1,0:T(8,128)(2,1)S(1)} collective-permute-done((bf16[128,1792]{1,0:T(8,128)(2,1)S(1)}, bf16[128,1792]{1,0:T(8,128)(2,1)S(1)}, u32[]{:S(2)}, u32[]{:S(2)}) %collective-permute-start.18) | collective-permute-done | bytes 458784 | tf_op jit(solution)/shard_map/ppermute | solution.py:42
  129.1 4.1 %all-to-all-start.1 = ((bf16[8,32,1792]{2,1,0:T(8,128)(2,1)}), bf16[8,32,1792]{2,1,0:T(8,128)(2,1)S(1)}, u32[]{:S(2)}, u32[]{:S(2)}) async-start(bf16[8,32,1792]{2,1,0:T(8,128)(2,1)} %pad_maximum_fusion.3), calls=%async_computation.1 | async-start | bytes 1835008 | tf_op jit(solution)/shard_map/all_to_all | solution.py:125
  133.2 4.2 %fusion.29 = (bf16[128,1792]{1,0:T(8,128)(2,1)}, bf16[128,1792]{1,0:T(8,128)(2,1)}, bf16[128,1792]{1,0:T(8,128)(2,1)}) fusion(bf16[128,1792]{1,0:T(8,128)(2,1)} %param.19, bf16[128,1792]{1,0:T(8,128)(2,1)} %param.18, bf16[128,1792]{1,0:T(8,128)(2,1)} %param.17, bf16[128,1792]{1,0:T(8,128)(2,1)} %collective-permute-done.21, bf16[512,1792]{1,0:T(8,128)(2,1)} %copy-done.3, ...), kind=kOutput, calls=%fused_computation.55 | convolution fusion | flops 239697920 | bytes 5177344 | tf_op jit(solution)/shard_map/dot_general | solution.py:33
  137.4 4.9 %collective-permute-done.20 = bf16[1792,256]{1,0:T(8,128)(2,1)} collective-permute-done((bf16[1792,256]{1,0:T(8,128)(2,1)}, bf16[1792,256]{1,0:T(8,128)(2,1)}, u32[]{:S(2)}, u32[]{:S(2)}) %collective-permute-start.20) | collective-permute-done | bytes 917536 | tf_op jit(solution)/shard_map/ppermute | solution.py:37
  142.3 1.9 %convolution_add_fusion = f32[1792,256]{1,0:T(8,128)S(1)} fusion(bf16[512,1792]{1,0:T(8,128)(2,1)S(1)} %constant_dynamic-update-slice_fusion.5, bf16[1792,256]{1,0:T(8,128)(2,1)} %collective-permute-done.20, bf16[512,512]{1,0:T(8,128)(2,1)S(1)} %maximum_select_fusion), kind=kOutput, calls=%fused_computation | convolution fusion | flops 470679552 | bytes 4849664 | tf_op jit(solution)/shard_map/dot_general | solution.py:33
  145.9 3.1 %fusion.27 = (bf16[2,1792,128]{2,1,0:T(8,128)(2,1)}, bf16[2,1792,128]{2,1,0:T(8,128)(2,1)}, bf16[2,1792,128]{2,1,0:T(8,128)(2,1)}) fusion(f32[1,1792,128]{2,1,0:T(8,128)S(1)} %get-tuple-element.44, f32[1,1792,128]{2,1,0:T(8,128)S(1)} %get-tuple-element.43, bf16[2,1792,128]{2,1,0:T(8,128)(2,1)S(1)} %copy-done.4, bf16[2,1792,128]{2,1,0:T(8,128)(2,1)S(1)} %copy-done.5, ...), kind=kLoop, calls=%fused_computation.50 | loop fusion | flops 9175040 | bytes 7340032 | tf_op jit(solution)/shard_map/convert_element_type | solution.py:28
  149.0 8.1 %all-to-all-done.1 = bf16[8,32,1792]{2,1,0:T(8,128)(2,1)S(1)} async-done(((bf16[8,32,1792]{2,1,0:T(8,128)(2,1)}), bf16[8,32,1792]{2,1,0:T(8,128)(2,1)S(1)}, u32[]{:S(2)}, u32[]{:S(2)}) %all-to-all-start.1) | async-done | bytes 917536 | tf_op jit(solution)/shard_map/all_to_all | solution.py:125
  (84 shorter events, 14.7 us)
Async XLA Ops:
  0.6 12.3 %copy-start.6 = (bf16[128,1792]{1,0:T(8,128)(2,1)S(1)}, bf16[128,1792]{1,0:T(8,128)(2,1)}, u32[]{:S(2)}) copy-start(bf16[128,1792]{1,0:T(8,128)(2,1)} %param.17) | copy-start | bytes 1376260
  0.6 12.3 %copy-start.1 = (bf16[2,1792,128]{2,1,0:T(8,128)(2,1)S(1)}, bf16[2,1792,128]{2,1,0:T(8,128)(2,1)}, u32[]{:S(2)}) copy-start(bf16[2,1792,128]{2,1,0:T(8,128)(2,1)} %param.14) | copy-start | bytes 2752516
  3.4 33.1 %all-to-all-start = ((bf16[8,32,1792]{2,1,0:T(8,128)(2,1)}), bf16[8,32,1792]{2,1,0:T(8,128)(2,1)S(1)}, u32[]{:S(2)}, u32[]{:S(2)}) async-start(bf16[8,32,1792]{2,1,0:T(8,128)(2,1)} %get-tuple-element.22), calls=%async_computation | async-start | bytes 1835008 | tf_op jit(solution)/shard_map/all_to_all | solution.py:125
  36.5 2.2 %copy-start = (bf16[1792,128]{1,0:T(8,128)(2,1)S(1)}, bf16[1792,128]{1,0:T(8,128)(2,1)}, u32[]{:S(2)}) copy-start(bf16[1792,128]{1,0:T(8,128)(2,1)} %get-tuple-element.26) | copy-start | bytes 1376260
  36.6 6.2 %copy-start.7 = (bf16[128,1792]{1,0:T(8,128)(2,1)S(1)}, bf16[128,1792]{1,0:T(8,128)(2,1)}, u32[]{:S(2)}) copy-start(bf16[128,1792]{1,0:T(8,128)(2,1)} %param.17) | copy-start | bytes 1376260
  36.6 10.8 %collective-permute-start = (bf16[128,1792]{1,0:T(8,128)(2,1)S(1)}, bf16[128,1792]{1,0:T(8,128)(2,1)S(1)}, u32[]{:S(2)}, u32[]{:S(2)}) collective-permute-start(bf16[128,1792]{1,0:T(8,128)(2,1)S(1)} %bitcast.36), channel_id=1, source_target_pairs={{0,1},{1,2},{2,3},{3,0},{4,5},{5,6},{6,7},{7,4},{8,9},{9,10},{10,1... | collective-permute-start | bytes 1376264 | tf_op jit(solution)/shard_map/ppermute | solution.py:42
  36.9 12.0 %collective-permute-start.2 = (bf16[128,1792]{1,0:T(8,128)(2,1)S(1)}, bf16[128,1792]{1,0:T(8,128)(2,1)S(1)}, u32[]{:S(2)}, u32[]{:S(2)}) collective-permute-start(bf16[128,1792]{1,0:T(8,128)(2,1)S(1)} %bitcast.37), channel_id=1, source_target_pairs={{0,3},{1,0},{2,1},{3,2},{4,7},{5,4},{6,5},{7,6},{8,11},{9,8},{10,9... | collective-permute-start | bytes 1376264 | tf_op jit(solution)/shard_map/ppermute | solution.py:42
  39.0 25.1 %collective-permute-start.1 = (bf16[1792,256]{1,0:T(8,128)(2,1)S(1)}, bf16[1792,256]{1,0:T(8,128)(2,1)S(1)}, u32[]{:S(2)}, u32[]{:S(2)}) collective-permute-start(bf16[1792,256]{1,0:T(8,128)(2,1)S(1)} %pad_maximum_fusion.1), channel_id=1, source_target_pairs={{0,4},{4,0},{1,5},{5,1},{2,6},{6,2},{3,7},{7,3},{8,12},{12,8},{9,1... | collective-permute-start | bytes 2752520 | tf_op jit(solution)/shard_map/ppermute | solution.py:37
  42.9 28.2 %collective-permute-start.7 = (bf16[128,1792]{1,0:T(8,128)(2,1)S(1)}, bf16[128,1792]{1,0:T(8,128)(2,1)S(1)}, u32[]{:S(2)}, u32[]{:S(2)}) collective-permute-start(bf16[128,1792]{1,0:T(8,128)(2,1)S(1)} %copy-done.7), channel_id=1, source_target_pairs={{0,4},{4,0},{1,5},{5,1},{2,6},{6,2},{3,7},{7,3},{8,12},{12,8},{9,1... | collective-permute-start | bytes 1376264 | tf_op jit(solution)/shard_map/ppermute | solution.py:37
  47.4 24.6 %collective-permute-start.11 = (bf16[128,1792]{1,0:T(8,128)(2,1)S(1)}, bf16[128,1792]{1,0:T(8,128)(2,1)S(1)}, u32[]{:S(2)}, u32[]{:S(2)}) collective-permute-start(bf16[128,1792]{1,0:T(8,128)(2,1)S(1)} %bitcast.32), channel_id=1, source_target_pairs={{0,1},{1,2},{2,3},{3,0},{4,5},{5,6},{6,7},{7,4},{8,9},{9,10},{10,1... | collective-permute-start | bytes 1376264 | tf_op jit(solution)/shard_map/ppermute | solution.py:42
  48.9 22.2 %collective-permute-start.12 = (bf16[128,1792]{1,0:T(8,128)(2,1)S(1)}, bf16[128,1792]{1,0:T(8,128)(2,1)S(1)}, u32[]{:S(2)}, u32[]{:S(2)}) collective-permute-start(bf16[128,1792]{1,0:T(8,128)(2,1)S(1)} %bitcast.33), channel_id=1, source_target_pairs={{0,3},{1,0},{2,1},{3,2},{4,7},{5,4},{6,5},{7,6},{8,11},{9,8},{10,9... | collective-permute-start | bytes 1376264 | tf_op jit(solution)/shard_map/ppermute | solution.py:42
  49.4 17.6 %collective-permute-start.3 = (bf16[128,1792]{1,0:T(8,128)(2,1)S(1)}, bf16[128,1792]{1,0:T(8,128)(2,1)S(1)}, u32[]{:S(2)}, u32[]{:S(2)}) collective-permute-start(bf16[128,1792]{1,0:T(8,128)(2,1)S(1)} %collective-permute-done), channel_id=1, source_target_pairs={{0,1},{1,2},{2,3},{3,0},{4,5},{5,6},{6,7},{7,4},{8,9},{9,10},{10,1... | collective-permute-start | bytes 1376264 | tf_op jit(solution)/shard_map/ppermute | solution.py:42
  67.7 4.3 %collective-permute-start.4 = (f32[256,512]{1,0:T(8,128)S(1)}, f32[256,512]{1,0:T(8,128)S(1)}, u32[]{:S(2)}, u32[]{:S(2)}) collective-permute-start(f32[256,512]{1,0:T(8,128)S(1)} %get-tuple-element.71), channel_id=1, source_target_pairs={{0,64},{64,0},{1,65},{65,1},{2,66},{66,2},{3,67},{67,3},{4,68},{68... | collective-permute-start | bytes 1572872 | tf_op jit(solution)/shard_map/ppermute | solution.py:37
  71.1 10.9 %collective-permute-start.13 = (bf16[128,1792]{1,0:T(8,128)(2,1)S(1)}, bf16[128,1792]{1,0:T(8,128)(2,1)S(1)}, u32[]{:S(2)}, u32[]{:S(2)}) collective-permute-start(bf16[128,1792]{1,0:T(8,128)(2,1)S(1)} %collective-permute-done.12), channel_id=1, source_target_pairs={{0,3},{1,0},{2,1},{3,2},{4,7},{5,4},{6,5},{7,6},{8,11},{9,8},{10,9... | collective-permute-start | bytes 1376264 | tf_op jit(solution)/shard_map/ppermute | solution.py:42
  72.2 8.0 %collective-permute-start.5 = (bf16[256,512]{1,0:T(8,128)(2,1)S(1)}, bf16[256,512]{1,0:T(8,128)(2,1)S(1)}, u32[]{:S(2)}, u32[]{:S(2)}) collective-permute-start(bf16[256,512]{1,0:T(8,128)(2,1)S(1)} %get-tuple-element.38), channel_id=1, source_target_pairs={{0,128},{128,0},{1,129},{129,1},{2,130},{130,2},{3,131},{131,3},{4... | collective-permute-start | bytes 786440 | tf_op jit(solution)/shard_map/ppermute | solution.py:37
  80.4 1.7 %collective-permute-start.6 = (bf16[256,256]{1,0:T(8,128)(2,1)S(1)}, bf16[256,256]{1,0:T(8,128)(2,1)S(1)}, u32[]{:S(2)}, u32[]{:S(2)}) collective-permute-start(bf16[256,256]{1,0:T(8,128)(2,1)S(1)} %get-tuple-element.65), channel_id=1, source_target_pairs={{0,64},{64,0},{1,65},{65,1},{2,66},{66,2},{3,67},{67,3},{4,68},{68... | collective-permute-start | bytes 393224 | tf_op jit(solution)/shard_map/ppermute | solution.py:37
  82.1 10.4 %copy-start.3 = (bf16[512,1792]{1,0:T(8,128)(2,1)}, bf16[512,1792]{1,0:T(8,128)(2,1)S(1)}, u32[]{:S(2)}) copy-start(bf16[512,1792]{1,0:T(8,128)(2,1)S(1)} %constant_dynamic-update-slice_fusion.9) | copy-start | bytes 5505028
  83.1 1.6 %collective-permute-start.14 = (f32[256,256]{1,0:T(8,128)S(1)}, f32[256,256]{1,0:T(8,128)S(1)}, u32[]{:S(2)}, u32[]{:S(2)}) collective-permute-start(f32[256,256]{1,0:T(8,128)S(1)} %get-tuple-element.73), channel_id=1, source_target_pairs={{0,64},{64,0},{1,65},{65,1},{2,66},{66,2},{3,67},{67,3},{4,68},{68... | collective-permute-start | bytes 786440 | tf_op jit(solution)/shard_map/ppermute | solution.py:37
  84.8 7.3 %collective-permute-start.15 = (bf16[256,256]{1,0:T(8,128)(2,1)S(1)}, bf16[256,256]{1,0:T(8,128)(2,1)S(1)}, u32[]{:S(2)}, u32[]{:S(2)}) collective-permute-start(bf16[256,256]{1,0:T(8,128)(2,1)S(1)} %get-tuple-element.36), channel_id=1, source_target_pairs={{0,128},{128,0},{1,129},{129,1},{2,130},{130,2},{3,131},{131,3},{4... | collective-permute-start | bytes 393224 | tf_op jit(solution)/shard_map/ppermute | solution.py:37
  88.1 27.4 %collective-permute-start.10 = (bf16[128,1792]{1,0:T(8,128)(2,1)S(1)}, bf16[128,1792]{1,0:T(8,128)(2,1)S(1)}, u32[]{:S(2)}, u32[]{:S(2)}) collective-permute-start(bf16[128,1792]{1,0:T(8,128)(2,1)S(1)} %get-tuple-element.46), channel_id=1, source_target_pairs={{0,3},{1,0},{2,1},{3,2},{4,7},{5,4},{6,5},{7,6},{8,11},{9,8},{10,9... | collective-permute-start | bytes 1376264 | tf_op jit(solution)/shard_map/ppermute | solution.py:42
  88.5 12.4 %collective-permute-start.8 = (bf16[128,1792]{1,0:T(8,128)(2,1)S(1)}, bf16[128,1792]{1,0:T(8,128)(2,1)S(1)}, u32[]{:S(2)}, u32[]{:S(2)}) collective-permute-start(bf16[128,1792]{1,0:T(8,128)(2,1)S(1)} %get-tuple-element.45), channel_id=1, source_target_pairs={{0,1},{1,2},{2,3},{3,0},{4,5},{5,6},{6,7},{7,4},{8,9},{9,10},{10,1... | collective-permute-start | bytes 1376264 | tf_op jit(solution)/shard_map/ppermute | solution.py:42
  92.4 5.4 %collective-permute-start.16 = (bf16[256,512]{1,0:T(8,128)(2,1)S(1)}, bf16[256,512]{1,0:T(8,128)(2,1)S(1)}, u32[]{:S(2)}, u32[]{:S(2)}) collective-permute-start(bf16[256,512]{1,0:T(8,128)(2,1)S(1)} %pad_maximum_fusion.6), channel_id=1, source_target_pairs={{0,64},{64,0},{1,65},{65,1},{2,66},{66,2},{3,67},{67,3},{4,68},{68... | collective-permute-start | bytes 786440 | tf_op jit(solution)/shard_map/ppermute | solution.py:37
  93.7 39.5 %collective-permute-start.21 = (bf16[128,1792]{1,0:T(8,128)(2,1)}, bf16[128,1792]{1,0:T(8,128)(2,1)}, u32[]{:S(2)}, u32[]{:S(2)}) collective-permute-start(bf16[128,1792]{1,0:T(8,128)(2,1)} %convolution_convert_fusion.2), channel_id=1, source_target_pairs={{0,4},{4,0},{1,5},{5,1},{2,6},{6,2},{3,7},{7,3},{8,12},{12,8},{9,1... | collective-permute-start | bytes 1376264 | tf_op jit(solution)/shard_map/ppermute | solution.py:37
  99.2 13.9 %collective-permute-start.17 = (bf16[128,1792]{1,0:T(8,128)(2,1)S(1)}, bf16[128,1792]{1,0:T(8,128)(2,1)S(1)}, u32[]{:S(2)}, u32[]{:S(2)}) collective-permute-start(bf16[128,1792]{1,0:T(8,128)(2,1)S(1)} %get-tuple-element.47), channel_id=1, source_target_pairs={{0,3},{1,0},{2,1},{3,2},{4,7},{5,4},{6,5},{7,6},{8,11},{9,8},{10,9... | collective-permute-start | bytes 1376264 | tf_op jit(solution)/shard_map/ppermute | solution.py:42
  101.0 14.7 %collective-permute-start.9 = (bf16[128,1792]{1,0:T(8,128)(2,1)S(1)}, bf16[128,1792]{1,0:T(8,128)(2,1)S(1)}, u32[]{:S(2)}, u32[]{:S(2)}) collective-permute-start(bf16[128,1792]{1,0:T(8,128)(2,1)S(1)} %fusion.11), channel_id=1, source_target_pairs={{0,1},{1,2},{2,3},{3,0},{4,5},{5,6},{6,7},{7,4},{8,9},{9,10},{10,1... | collective-permute-start | bytes 1376264 | tf_op jit(solution)/shard_map/ppermute | solution.py:42
  104.8 18.4 %collective-permute-start.19 = (bf16[128,1792]{1,0:T(8,128)(2,1)S(1)}, bf16[128,1792]{1,0:T(8,128)(2,1)S(1)}, u32[]{:S(2)}, u32[]{:S(2)}) collective-permute-start(bf16[128,1792]{1,0:T(8,128)(2,1)S(1)} %get-tuple-element.48), channel_id=1, source_target_pairs={{0,1},{1,2},{2,3},{3,0},{4,5},{5,6},{6,7},{7,4},{8,9},{9,10},{10,1... | collective-permute-start | bytes 1376264 | tf_op jit(solution)/shard_map/ppermute | solution.py:42
  113.1 29.1 %collective-permute-start.20 = (bf16[1792,256]{1,0:T(8,128)(2,1)}, bf16[1792,256]{1,0:T(8,128)(2,1)}, u32[]{:S(2)}, u32[]{:S(2)}) collective-permute-start(bf16[1792,256]{1,0:T(8,128)(2,1)} %convolution_convert_fusion), channel_id=1, source_target_pairs={{0,4},{4,0},{1,5},{5,1},{2,6},{6,2},{3,7},{7,3},{8,12},{12,8},{9,1... | collective-permute-start | bytes 2752520 | tf_op jit(solution)/shard_map/ppermute | solution.py:37
  115.5 12.4 %collective-permute-start.18 = (bf16[128,1792]{1,0:T(8,128)(2,1)S(1)}, bf16[128,1792]{1,0:T(8,128)(2,1)S(1)}, u32[]{:S(2)}, u32[]{:S(2)}) collective-permute-start(bf16[128,1792]{1,0:T(8,128)(2,1)S(1)} %fusion.8), channel_id=1, source_target_pairs={{0,3},{1,0},{2,1},{3,2},{4,7},{5,4},{6,5},{7,6},{8,11},{9,8},{10,9... | collective-permute-start | bytes 1376264 | tf_op jit(solution)/shard_map/ppermute | solution.py:42
  129.1 28.0 %all-to-all-start.1 = ((bf16[8,32,1792]{2,1,0:T(8,128)(2,1)}), bf16[8,32,1792]{2,1,0:T(8,128)(2,1)S(1)}, u32[]{:S(2)}, u32[]{:S(2)}) async-start(bf16[8,32,1792]{2,1,0:T(8,128)(2,1)} %pad_maximum_fusion.3), calls=%async_computation.1 | async-start | bytes 1835008 | tf_op jit(solution)/shard_map/all_to_all | solution.py:125
  144.2 1.4 copy-start.4
  144.2 1.7 %copy-start.5 = (bf16[2,1792,128]{2,1,0:T(8,128)(2,1)S(1)}, bf16[2,1792,128]{2,1,0:T(8,128)(2,1)}, u32[]{:S(2)}) copy-start(bf16[2,1792,128]{2,1,0:T(8,128)(2,1)} %param.15) | copy-start | bytes 2752516
  145.9 11.2 %copy-start.8 = (bf16[8,32,256]{2,1,0:T(8,128)(2,1)S(1)}, bf16[8,32,256]{2,1,0:T(8,128)(2,1)}, u32[]{:S(2)}) copy-start(bf16[8,32,256]{2,1,0:T(8,128)(2,1)} %get-tuple-element.23) | copy-start | bytes 393220
  (1 other events, 1.2 us)

commit v4 on v3

--- a/solution.py
+++ b/solution.py
@@ -184,16 +184,18 @@
     silu_gate = gate_pre * sigmoid_gate
     scaled = core_gather(to_bf16(silu_gate * up_pre))
 
-    def scatter_x(value, step):
+    def scatter_x(value, step, earlier=None):
         chunks = [value[i * rows : (i + 1) * rows] for i in range(4)]
         near, back_near = (chunks[2], chunks[1]) if step == 1 else (chunks[1], chunks[2])
         across = shift(to_bf16(chunks[3]), step).astype(jnp.float32)
         other = shift(to_bf16(back_near), -step).astype(jnp.float32)
+        if earlier is not None:
+            across = after(across, earlier)
         one = shift(to_bf16(near + across), step).astype(jnp.float32)
-        return to_bf16(chunks[0] + one + other)
+        return to_bf16(chunks[0] + one + other), other
 
     mixed_part = f32_dot(scaled, downs, ((1,), (0,)))
-    mixed_sum = scatter_x(mixed_part, 1)
+    mixed_sum, mixed_near = scatter_x(mixed_part, 1)
 
     grad_low = after(grad_low, scaled)
     back = y_sum(
@@ -209,7 +211,8 @@
             (d_gate[:, :hidden], d_up[:, :hidden], d_gate[:, hidden:], d_up[:, hidden:]), axis=1
         )
     )
-    delta_sum = scatter_x(f32_dot(d_paired, paired, ((1,), (1,))), -1)
+    delta_part = f32_dot(d_paired, paired, ((1,), (1,)))
+    delta_sum = scatter_x(delta_part, -1, mixed_near)[0]
     returned = exchange(interleave(mixed_sum, delta_sum))
 
     grad_down_far = to_bf16(f32_dot(scaled[:, hidden:], grad_all, ((0,), (0,))))

time: 159 us -> 160 us (level)
    ppermute x10, starting transfers between devices: 17.1 us -> 18.9 us  [swap(): return lax.ppermute(value, axis, [(0, 1), (1, 0)])]
  transfers between devices with their start and end apart: 24 -> 24, of which waited for: 16 -> 15; matrix products, arithmetic and copies ran while one was open for 12% -> 12% of each run, Pallas kernels for 0% -> 0%
where the time goes in v4:
time: 160 us
  waiting for transfers between devices  87 us (54%)
  starting transfers between devices  46 us (29%)
  matrix products  13.2 us (8%)
  other arithmetic  5.76 us (4%)
  local copies, waits for them, and re-layouts  4.38 us (3%)
  Pallas kernels  2.75 us (2%)
    all_to_all x2, waiting for transfers between devices, exchange(): lax.all_to_all(pair, ('y_lo', 'z_hi'), split_axis=0, concat_axis=0, tiled...  30.3 us
    ppermute x12, waiting for transfers between devices, shift(): lax.ppermute(value, 'x', [(i, (i + step) % size) for i in range(size)])  28.7 us
    ppermute x10, waiting for transfers between devices, swap(): return lax.ppermute(value, axis, [(0, 1), (1, 0)])  28 us
    ppermute x10, starting transfers between devices, swap(): return lax.ppermute(value, axis, [(0, 1), (1, 0)])  18.9 us
    all_to_all x2, starting transfers between devices, exchange(): lax.all_to_all(pair, ('y_lo', 'z_hi'), split_axis=0, concat_axis=0, tiled...  13.6 us
    ppermute x12, starting transfers between devices, shift(): lax.ppermute(value, 'x', [(i, (i + step) % size) for i in range(size)])  13.4 us
    dot_general x11, matrix products, f32_dot(): lax.dot_general(left, right, (dims, ((), ())), preferred_element_type=jnp...  13.2 us
  transfers between devices with their start and end apart: 24, of which 15 were waited for; matrix products, arithmetic and copies ran while one was open for 12% of the time, Pallas kernels for 0%

profile of v4, /device:TPU:6, one launch (start us, length us, event | category | flops | bytes accessed | tf_op | source)
XLA Modules:
  0.0 160.2 jit_solution(2296590201461591555)
XLA Ops:
  0.7 2.7 %dispatch.1 = (bf16[8,32,1792]{2,1,0:T(8,128)(2,1)}, bf16[8,32,256]{2,1,0:T(8,128)(2,1)}) custom-call(s32[8,128]{1,0:T(8,128)} %bitcast.43, bf16[8,128]{1,0:T(8,128)(2,1)} %bitcast.44, bf16[128,1792]{1,0:T(8,128)(2,1)} %tokens_ref.1, bf16[128,1792]{1,0:T(8,128)(2,1)} %grads_ref.1), custom_call_target="tpu_custom_call" | custom-call | tf_op jit(solution)/shard_map/dispatch/pallas_call | solution.py:110
  3.4 9.5 %all-to-all-start = ((bf16[8,32,1792]{2,1,0:T(8,128)(2,1)}), bf16[8,32,1792]{2,1,0:T(8,128)(2,1)S(1)}, u32[]{:S(2)}, u32[]{:S(2)}) async-start(bf16[8,32,1792]{2,1,0:T(8,128)(2,1)} %get-tuple-element.23), calls=%async_computation | async-start | bytes 1835008 | tf_op jit(solution)/shard_map/all_to_all | solution.py:125
  13.8 22.8 %all-to-all-done = bf16[8,32,1792]{2,1,0:T(8,128)(2,1)S(1)} async-done(((bf16[8,32,1792]{2,1,0:T(8,128)(2,1)}), bf16[8,32,1792]{2,1,0:T(8,128)(2,1)S(1)}, u32[]{:S(2)}, u32[]{:S(2)}) %all-to-all-start) | async-done | bytes 917536 | tf_op jit(solution)/shard_map/all_to_all | solution.py:125
  36.9 1.8 %collective-permute-start.2 = (bf16[128,1792]{1,0:T(8,128)(2,1)S(1)}, bf16[128,1792]{1,0:T(8,128)(2,1)S(1)}, u32[]{:S(2)}, u32[]{:S(2)}) collective-permute-start(bf16[128,1792]{1,0:T(8,128)(2,1)S(1)} %bitcast.37), channel_id=1, source_target_pairs={{0,3},{1,0},{2,1},{3,2},{4,7},{5,4},{6,5},{7,6},{8,11},{9,8},{10,9... | collective-permute-start | bytes 1376264 | tf_op jit(solution)/shard_map/ppermute | solution.py:42
  39.0 3.9 %collective-permute-start.1 = (bf16[1792,256]{1,0:T(8,128)(2,1)S(1)}, bf16[1792,256]{1,0:T(8,128)(2,1)S(1)}, u32[]{:S(2)}, u32[]{:S(2)}) collective-permute-start(bf16[1792,256]{1,0:T(8,128)(2,1)S(1)} %pad_maximum_fusion.1), channel_id=1, source_target_pairs={{0,4},{4,0},{1,5},{5,1},{2,6},{6,2},{3,7},{7,3},{8,12},{12,8},{9,1... | collective-permute-start | bytes 2752520 | tf_op jit(solution)/shard_map/ppermute | solution.py:37
  43.1 4.3 %collective-permute-done = bf16[128,1792]{1,0:T(8,128)(2,1)S(1)} collective-permute-done((bf16[128,1792]{1,0:T(8,128)(2,1)S(1)}, bf16[128,1792]{1,0:T(8,128)(2,1)S(1)}, u32[]{:S(2)}, u32[]{:S(2)}) %collective-permute-start) | collective-permute-done | bytes 458784 | tf_op jit(solution)/shard_map/ppermute | solution.py:42
  47.4 1.5 collective-permute-start.11
  49.4 2.7 %collective-permute-start.3 = (bf16[128,1792]{1,0:T(8,128)(2,1)S(1)}, bf16[128,1792]{1,0:T(8,128)(2,1)S(1)}, u32[]{:S(2)}, u32[]{:S(2)}) collective-permute-start(bf16[128,1792]{1,0:T(8,128)(2,1)S(1)} %collective-permute-done), channel_id=1, source_target_pairs={{0,1},{1,2},{2,3},{3,0},{4,5},{5,6},{6,7},{7,4},{8,9},{9,10},{10,1... | collective-permute-start | bytes 1376264 | tf_op jit(solution)/shard_map/ppermute | solution.py:42
  52.2 11.9 %collective-permute-done.1 = bf16[1792,256]{1,0:T(8,128)(2,1)S(1)} collective-permute-done((bf16[1792,256]{1,0:T(8,128)(2,1)S(1)}, bf16[1792,256]{1,0:T(8,128)(2,1)S(1)}, u32[]{:S(2)}, u32[]{:S(2)}) %collective-permute-start.1) | collective-permute-done | bytes 917536 | tf_op jit(solution)/shard_map/ppermute | solution.py:37
  64.8 2.2 %collective-permute-done.3 = bf16[128,1792]{1,0:T(8,128)(2,1)S(1)} collective-permute-done((bf16[128,1792]{1,0:T(8,128)(2,1)S(1)}, bf16[128,1792]{1,0:T(8,128)(2,1)S(1)}, u32[]{:S(2)}, u32[]{:S(2)}) %collective-permute-start.3) | collective-permute-done | bytes 458784 | tf_op jit(solution)/shard_map/ppermute | solution.py:42
  67.8 3.3 %collective-permute-done.7 = bf16[128,1792]{1,0:T(8,128)(2,1)S(1)} collective-permute-done((bf16[128,1792]{1,0:T(8,128)(2,1)S(1)}, bf16[128,1792]{1,0:T(8,128)(2,1)S(1)}, u32[]{:S(2)}, u32[]{:S(2)}) %collective-permute-start.7) | collective-permute-done | bytes 458784 | tf_op jit(solution)/shard_map/ppermute | solution.py:37
  72.2 3.1 %collective-permute-start.5 = (bf16[256,512]{1,0:T(8,128)(2,1)S(1)}, bf16[256,512]{1,0:T(8,128)(2,1)S(1)}, u32[]{:S(2)}, u32[]{:S(2)}) collective-permute-start(bf16[256,512]{1,0:T(8,128)(2,1)S(1)} %get-tuple-element.40), channel_id=1, source_target_pairs={{0,128},{128,0},{1,129},{129,1},{2,130},{130,2},{3,131},{131,3},{4... | collective-permute-start | bytes 786440 | tf_op jit(solution)/shard_map/ppermute | solution.py:37
  75.4 4.8 %collective-permute-done.5 = bf16[256,512]{1,0:T(8,128)(2,1)S(1)} collective-permute-done((bf16[256,512]{1,0:T(8,128)(2,1)S(1)}, bf16[256,512]{1,0:T(8,128)(2,1)S(1)}, u32[]{:S(2)}, u32[]{:S(2)}) %collective-permute-start.5) | collective-permute-done | bytes 262176 | tf_op jit(solution)/shard_map/ppermute | solution.py:37
  80.5 1.5 collective-permute-done.13
  84.8 3.3 %collective-permute-start.15 = (bf16[256,256]{1,0:T(8,128)(2,1)S(1)}, bf16[256,256]{1,0:T(8,128)(2,1)S(1)}, u32[]{:S(2)}, u32[]{:S(2)}) collective-permute-start(bf16[256,256]{1,0:T(8,128)(2,1)S(1)} %get-tuple-element.38), channel_id=1, source_target_pairs={{0,128},{128,0},{1,129},{129,1},{2,130},{130,2},{3,131},{131,3},{4... | collective-permute-start | bytes 393224 | tf_op jit(solution)/shard_map/ppermute | solution.py:37
  88.1 2.2 %collective-permute-start.8 = (bf16[128,1792]{1,0:T(8,128)(2,1)S(1)}, bf16[128,1792]{1,0:T(8,128)(2,1)S(1)}, u32[]{:S(2)}, u32[]{:S(2)}) collective-permute-start(bf16[128,1792]{1,0:T(8,128)(2,1)S(1)} %get-tuple-element.48), channel_id=1, source_target_pairs={{0,1},{1,2},{2,3},{3,0},{4,5},{5,6},{6,7},{7,4},{8,9},{9,10},{10,1... | collective-permute-start | bytes 1376264 | tf_op jit(solution)/shard_map/ppermute | solution.py:42
  90.3 1.8 %collective-permute-done.15 = bf16[256,256]{1,0:T(8,128)(2,1)S(1)} collective-permute-done((bf16[256,256]{1,0:T(8,128)(2,1)S(1)}, bf16[256,256]{1,0:T(8,128)(2,1)S(1)}, u32[]{:S(2)}, u32[]{:S(2)}) %collective-permute-start.15) | collective-permute-done | bytes 131104 | tf_op jit(solution)/shard_map/ppermute | solution.py:37
  92.5 1.2 convolution_convert_fusion.2
  93.7 4.1 %collective-permute-start.21 = (bf16[128,1792]{1,0:T(8,128)(2,1)}, bf16[128,1792]{1,0:T(8,128)(2,1)}, u32[]{:S(2)}, u32[]{:S(2)}) collective-permute-start(bf16[128,1792]{1,0:T(8,128)(2,1)} %convolution_convert_fusion.2), channel_id=1, source_target_pairs={{0,4},{4,0},{1,5},{5,1},{2,6},{6,2},{3,7},{7,3},{8,12},{12,8},{9,1... | collective-permute-start | bytes 1376264 | tf_op jit(solution)/shard_map/ppermute | solution.py:37
  98.0 1.1 fusion.46
  100.5 3.4 %collective-permute-start.9 = (bf16[128,1792]{1,0:T(8,128)(2,1)S(1)}, bf16[128,1792]{1,0:T(8,128)(2,1)S(1)}, u32[]{:S(2)}, u32[]{:S(2)}) collective-permute-start(bf16[128,1792]{1,0:T(8,128)(2,1)S(1)} %fusion.11), channel_id=1, source_target_pairs={{0,1},{1,2},{2,3},{3,0},{4,5},{5,6},{6,7},{7,4},{8,9},{9,10},{10,1... | collective-permute-start | bytes 1376264 | tf_op jit(solution)/shard_map/ppermute | solution.py:42
  104.0 1.6 %convolution_convert_fusion = bf16[1792,256]{1,0:T(8,128)(2,1)} fusion(bf16[512,1792]{1,0:T(8,128)(2,1)S(1)} %constant_dynamic-update-slice_fusion.5, bf16[512,512]{1,0:T(8,128)(2,1)S(1)} %maximum_select_fusion), kind=kOutput, calls=%fused_computation.2 | convolution fusion | flops 470220800 | bytes 3014656 | tf_op jit(solution)/shard_map/dot_general | solution.py:33
  105.6 7.7 %collective-permute-done.17 = bf16[128,1792]{1,0:T(8,128)(2,1)S(1)} collective-permute-done((bf16[128,1792]{1,0:T(8,128)(2,1)S(1)}, bf16[128,1792]{1,0:T(8,128)(2,1)S(1)}, u32[]{:S(2)}, u32[]{:S(2)}) %collective-permute-start.17) | collective-permute-done | bytes 458784 | tf_op jit(solution)/shard_map/ppermute | solution.py:42
  113.3 4.2 %collective-permute-start.20 = (bf16[1792,256]{1,0:T(8,128)(2,1)}, bf16[1792,256]{1,0:T(8,128)(2,1)}, u32[]{:S(2)}, u32[]{:S(2)}) collective-permute-start(bf16[1792,256]{1,0:T(8,128)(2,1)} %convolution_convert_fusion), channel_id=1, source_target_pairs={{0,4},{4,0},{1,5},{5,1},{2,6},{6,2},{3,7},{7,3},{8,12},{12,8},{9,1... | collective-permute-start | bytes 2752520 | tf_op jit(solution)/shard_map/ppermute | solution.py:37
  117.9 4.8 %collective-permute-done.19 = bf16[128,1792]{1,0:T(8,128)(2,1)S(1)} collective-permute-done((bf16[128,1792]{1,0:T(8,128)(2,1)S(1)}, bf16[128,1792]{1,0:T(8,128)(2,1)S(1)}, u32[]{:S(2)}, u32[]{:S(2)}) %collective-permute-start.19) | collective-permute-done | bytes 458784 | tf_op jit(solution)/shard_map/ppermute | solution.py:42
  122.7 7.1 %collective-permute-done.18 = bf16[128,1792]{1,0:T(8,128)(2,1)S(1)} collective-permute-done((bf16[128,1792]{1,0:T(8,128)(2,1)S(1)}, bf16[128,1792]{1,0:T(8,128)(2,1)S(1)}, u32[]{:S(2)}, u32[]{:S(2)}) %collective-permute-start.18) | collective-permute-done | bytes 458784 | tf_op jit(solution)/shard_map/ppermute | solution.py:42
  131.0 4.1 %all-to-all-start.1 = ((bf16[8,32,1792]{2,1,0:T(8,128)(2,1)}), bf16[8,32,1792]{2,1,0:T(8,128)(2,1)S(1)}, u32[]{:S(2)}, u32[]{:S(2)}) async-start(bf16[8,32,1792]{2,1,0:T(8,128)(2,1)} %pad_maximum_fusion.3), calls=%async_computation.1 | async-start | bytes 1835008 | tf_op jit(solution)/shard_map/all_to_all | solution.py:125
  135.1 4.2 %fusion.29 = (bf16[128,1792]{1,0:T(8,128)(2,1)}, bf16[128,1792]{1,0:T(8,128)(2,1)}, bf16[128,1792]{1,0:T(8,128)(2,1)}) fusion(bf16[128,1792]{1,0:T(8,128)(2,1)} %param.19, bf16[128,1792]{1,0:T(8,128)(2,1)} %param.18, bf16[128,1792]{1,0:T(8,128)(2,1)} %param.17, bf16[128,1792]{1,0:T(8,128)(2,1)} %collective-permute-done.21, bf16[512,1792]{1,0:T(8,128)(2,1)} %copy-done.3, ...), kind=kOutput, calls=%fused_computation.55 | convolution fusion | flops 239697920 | bytes 5177344 | tf_op jit(solution)/shard_map/dot_general | solution.py:33
  139.3 5.3 %collective-permute-done.20 = bf16[1792,256]{1,0:T(8,128)(2,1)} collective-permute-done((bf16[1792,256]{1,0:T(8,128)(2,1)}, bf16[1792,256]{1,0:T(8,128)(2,1)}, u32[]{:S(2)}, u32[]{:S(2)}) %collective-permute-start.20) | collective-permute-done | bytes 917536 | tf_op jit(solution)/shard_map/ppermute | solution.py:37
  144.6 1.9 %convolution_add_fusion = f32[1792,256]{1,0:T(8,128)S(1)} fusion(bf16[512,1792]{1,0:T(8,128)(2,1)S(1)} %constant_dynamic-update-slice_fusion.5, bf16[1792,256]{1,0:T(8,128)(2,1)} %collective-permute-done.20, bf16[512,512]{1,0:T(8,128)(2,1)S(1)} %maximum_select_fusion), kind=kOutput, calls=%fused_computation | convolution fusion | flops 470679552 | bytes 4849664 | tf_op jit(solution)/shard_map/dot_general | solution.py:33
  148.2 3.1 %fusion.27 = (bf16[2,1792,128]{2,1,0:T(8,128)(2,1)}, bf16[2,1792,128]{2,1,0:T(8,128)(2,1)}, bf16[2,1792,128]{2,1,0:T(8,128)(2,1)}) fusion(f32[1,1792,128]{2,1,0:T(8,128)S(1)} %get-tuple-element.46, f32[1,1792,128]{2,1,0:T(8,128)S(1)} %get-tuple-element.45, bf16[2,1792,128]{2,1,0:T(8,128)(2,1)S(1)} %copy-done.4, bf16[2,1792,128]{2,1,0:T(8,128)(2,1)S(1)} %copy-done.5, ...), kind=kLoop, calls=%fused_computation.50 | loop fusion | flops 9175040 | bytes 7340032 | tf_op jit(solution)/shard_map/convert_element_type | solution.py:28
  151.3 7.5 %all-to-all-done.1 = bf16[8,32,1792]{2,1,0:T(8,128)(2,1)S(1)} async-done(((bf16[8,32,1792]{2,1,0:T(8,128)(2,1)}), bf16[8,32,1792]{2,1,0:T(8,128)(2,1)S(1)}, u32[]{:S(2)}, u32[]{:S(2)}) %all-to-all-start.1) | async-done | bytes 917536 | tf_op jit(solution)/shard_map/all_to_all | solution.py:125
  (85 shorter events, 14.7 us)
Async XLA Ops:
  0.6 12.3 %copy-start.6 = (bf16[128,1792]{1,0:T(8,128)(2,1)S(1)}, bf16[128,1792]{1,0:T(8,128)(2,1)}, u32[]{:S(2)}) copy-start(bf16[128,1792]{1,0:T(8,128)(2,1)} %param.17) | copy-start | bytes 1376260
  0.6 12.3 %copy-start.1 = (bf16[2,1792,128]{2,1,0:T(8,128)(2,1)S(1)}, bf16[2,1792,128]{2,1,0:T(8,128)(2,1)}, u32[]{:S(2)}) copy-start(bf16[2,1792,128]{2,1,0:T(8,128)(2,1)} %param.14) | copy-start | bytes 2752516
  3.4 33.1 %all-to-all-start = ((bf16[8,32,1792]{2,1,0:T(8,128)(2,1)}), bf16[8,32,1792]{2,1,0:T(8,128)(2,1)S(1)}, u32[]{:S(2)}, u32[]{:S(2)}) async-start(bf16[8,32,1792]{2,1,0:T(8,128)(2,1)} %get-tuple-element.23), calls=%async_computation | async-start | bytes 1835008 | tf_op jit(solution)/shard_map/all_to_all | solution.py:125
  36.5 2.2 %copy-start = (bf16[1792,128]{1,0:T(8,128)(2,1)S(1)}, bf16[1792,128]{1,0:T(8,128)(2,1)}, u32[]{:S(2)}) copy-start(bf16[1792,128]{1,0:T(8,128)(2,1)} %get-tuple-element.27) | copy-start | bytes 1376260
  36.6 6.2 %copy-start.7 = (bf16[128,1792]{1,0:T(8,128)(2,1)S(1)}, bf16[128,1792]{1,0:T(8,128)(2,1)}, u32[]{:S(2)}) copy-start(bf16[128,1792]{1,0:T(8,128)(2,1)} %param.17) | copy-start | bytes 1376260
  36.6 10.8 %collective-permute-start = (bf16[128,1792]{1,0:T(8,128)(2,1)S(1)}, bf16[128,1792]{1,0:T(8,128)(2,1)S(1)}, u32[]{:S(2)}, u32[]{:S(2)}) collective-permute-start(bf16[128,1792]{1,0:T(8,128)(2,1)S(1)} %bitcast.36), channel_id=1, source_target_pairs={{0,1},{1,2},{2,3},{3,0},{4,5},{5,6},{6,7},{7,4},{8,9},{9,10},{10,1... | collective-permute-start | bytes 1376264 | tf_op jit(solution)/shard_map/ppermute | solution.py:42
  36.9 12.0 %collective-permute-start.2 = (bf16[128,1792]{1,0:T(8,128)(2,1)S(1)}, bf16[128,1792]{1,0:T(8,128)(2,1)S(1)}, u32[]{:S(2)}, u32[]{:S(2)}) collective-permute-start(bf16[128,1792]{1,0:T(8,128)(2,1)S(1)} %bitcast.37), channel_id=1, source_target_pairs={{0,3},{1,0},{2,1},{3,2},{4,7},{5,4},{6,5},{7,6},{8,11},{9,8},{10,9... | collective-permute-start | bytes 1376264 | tf_op jit(solution)/shard_map/ppermute | solution.py:42
  39.0 25.1 %collective-permute-start.1 = (bf16[1792,256]{1,0:T(8,128)(2,1)S(1)}, bf16[1792,256]{1,0:T(8,128)(2,1)S(1)}, u32[]{:S(2)}, u32[]{:S(2)}) collective-permute-start(bf16[1792,256]{1,0:T(8,128)(2,1)S(1)} %pad_maximum_fusion.1), channel_id=1, source_target_pairs={{0,4},{4,0},{1,5},{5,1},{2,6},{6,2},{3,7},{7,3},{8,12},{12,8},{9,1... | collective-permute-start | bytes 2752520 | tf_op jit(solution)/shard_map/ppermute | solution.py:37
  42.9 28.2 %collective-permute-start.7 = (bf16[128,1792]{1,0:T(8,128)(2,1)S(1)}, bf16[128,1792]{1,0:T(8,128)(2,1)S(1)}, u32[]{:S(2)}, u32[]{:S(2)}) collective-permute-start(bf16[128,1792]{1,0:T(8,128)(2,1)S(1)} %copy-done.7), channel_id=1, source_target_pairs={{0,4},{4,0},{1,5},{5,1},{2,6},{6,2},{3,7},{7,3},{8,12},{12,8},{9,1... | collective-permute-start | bytes 1376264 | tf_op jit(solution)/shard_map/ppermute | solution.py:37
  47.4 24.6 %collective-permute-start.11 = (bf16[128,1792]{1,0:T(8,128)(2,1)S(1)}, bf16[128,1792]{1,0:T(8,128)(2,1)S(1)}, u32[]{:S(2)}, u32[]{:S(2)}) collective-permute-start(bf16[128,1792]{1,0:T(8,128)(2,1)S(1)} %bitcast.32), channel_id=1, source_target_pairs={{0,1},{1,2},{2,3},{3,0},{4,5},{5,6},{6,7},{7,4},{8,9},{9,10},{10,1... | collective-permute-start | bytes 1376264 | tf_op jit(solution)/shard_map/ppermute | solution.py:42
  48.9 22.2 %collective-permute-start.12 = (bf16[128,1792]{1,0:T(8,128)(2,1)S(1)}, bf16[128,1792]{1,0:T(8,128)(2,1)S(1)}, u32[]{:S(2)}, u32[]{:S(2)}) collective-permute-start(bf16[128,1792]{1,0:T(8,128)(2,1)S(1)} %bitcast.33), channel_id=1, source_target_pairs={{0,3},{1,0},{2,1},{3,2},{4,7},{5,4},{6,5},{7,6},{8,11},{9,8},{10,9... | collective-permute-start | bytes 1376264 | tf_op jit(solution)/shard_map/ppermute | solution.py:42
  49.4 17.6 %collective-permute-start.3 = (bf16[128,1792]{1,0:T(8,128)(2,1)S(1)}, bf16[128,1792]{1,0:T(8,128)(2,1)S(1)}, u32[]{:S(2)}, u32[]{:S(2)}) collective-permute-start(bf16[128,1792]{1,0:T(8,128)(2,1)S(1)} %collective-permute-done), channel_id=1, source_target_pairs={{0,1},{1,2},{2,3},{3,0},{4,5},{5,6},{6,7},{7,4},{8,9},{9,10},{10,1... | collective-permute-start | bytes 1376264 | tf_op jit(solution)/shard_map/ppermute | solution.py:42
  67.7 4.3 %collective-permute-start.4 = (f32[256,512]{1,0:T(8,128)S(1)}, f32[256,512]{1,0:T(8,128)S(1)}, u32[]{:S(2)}, u32[]{:S(2)}) collective-permute-start(f32[256,512]{1,0:T(8,128)S(1)} %get-tuple-element.73), channel_id=1, source_target_pairs={{0,64},{64,0},{1,65},{65,1},{2,66},{66,2},{3,67},{67,3},{4,68},{68... | collective-permute-start | bytes 1572872 | tf_op jit(solution)/shard_map/ppermute | solution.py:37
  71.1 10.9 %collective-permute-start.13 = (bf16[128,1792]{1,0:T(8,128)(2,1)S(1)}, bf16[128,1792]{1,0:T(8,128)(2,1)S(1)}, u32[]{:S(2)}, u32[]{:S(2)}) collective-permute-start(bf16[128,1792]{1,0:T(8,128)(2,1)S(1)} %collective-permute-done.12), channel_id=1, source_target_pairs={{0,3},{1,0},{2,1},{3,2},{4,7},{5,4},{6,5},{7,6},{8,11},{9,8},{10,9... | collective-permute-start | bytes 1376264 | tf_op jit(solution)/shard_map/ppermute | solution.py:42
  72.2 8.0 %collective-permute-start.5 = (bf16[256,512]{1,0:T(8,128)(2,1)S(1)}, bf16[256,512]{1,0:T(8,128)(2,1)S(1)}, u32[]{:S(2)}, u32[]{:S(2)}) collective-permute-start(bf16[256,512]{1,0:T(8,128)(2,1)S(1)} %get-tuple-element.40), channel_id=1, source_target_pairs={{0,128},{128,0},{1,129},{129,1},{2,130},{130,2},{3,131},{131,3},{4... | collective-permute-start | bytes 786440 | tf_op jit(solution)/shard_map/ppermute | solution.py:37
  80.4 1.7 %collective-permute-start.6 = (bf16[256,256]{1,0:T(8,128)(2,1)S(1)}, bf16[256,256]{1,0:T(8,128)(2,1)S(1)}, u32[]{:S(2)}, u32[]{:S(2)}) collective-permute-start(bf16[256,256]{1,0:T(8,128)(2,1)S(1)} %get-tuple-element.67), channel_id=1, source_target_pairs={{0,64},{64,0},{1,65},{65,1},{2,66},{66,2},{3,67},{67,3},{4,68},{68... | collective-permute-start | bytes 393224 | tf_op jit(solution)/shard_map/ppermute | solution.py:37
  82.1 10.4 %copy-start.3 = (bf16[512,1792]{1,0:T(8,128)(2,1)}, bf16[512,1792]{1,0:T(8,128)(2,1)S(1)}, u32[]{:S(2)}) copy-start(bf16[512,1792]{1,0:T(8,128)(2,1)S(1)} %constant_dynamic-update-slice_fusion.9) | copy-start | bytes 5505028
  83.1 1.6 %collective-permute-start.14 = (f32[256,256]{1,0:T(8,128)S(1)}, f32[256,256]{1,0:T(8,128)S(1)}, u32[]{:S(2)}, u32[]{:S(2)}) collective-permute-start(f32[256,256]{1,0:T(8,128)S(1)} %get-tuple-element.75), channel_id=1, source_target_pairs={{0,64},{64,0},{1,65},{65,1},{2,66},{66,2},{3,67},{67,3},{4,68},{68... | collective-permute-start | bytes 786440 | tf_op jit(solution)/shard_map/ppermute | solution.py:37
  84.8 7.3 %collective-permute-start.15 = (bf16[256,256]{1,0:T(8,128)(2,1)S(1)}, bf16[256,256]{1,0:T(8,128)(2,1)S(1)}, u32[]{:S(2)}, u32[]{:S(2)}) collective-permute-start(bf16[256,256]{1,0:T(8,128)(2,1)S(1)} %get-tuple-element.38), channel_id=1, source_target_pairs={{0,128},{128,0},{1,129},{129,1},{2,130},{130,2},{3,131},{131,3},{4... | collective-permute-start | bytes 393224 | tf_op jit(solution)/shard_map/ppermute | solution.py:37
  88.1 12.4 %collective-permute-start.8 = (bf16[128,1792]{1,0:T(8,128)(2,1)S(1)}, bf16[128,1792]{1,0:T(8,128)(2,1)S(1)}, u32[]{:S(2)}, u32[]{:S(2)}) collective-permute-start(bf16[128,1792]{1,0:T(8,128)(2,1)S(1)} %get-tuple-element.48), channel_id=1, source_target_pairs={{0,1},{1,2},{2,3},{3,0},{4,5},{5,6},{6,7},{7,4},{8,9},{9,10},{10,1... | collective-permute-start | bytes 1376264 | tf_op jit(solution)/shard_map/ppermute | solution.py:42
  90.3 27.4 %collective-permute-start.10 = (bf16[128,1792]{1,0:T(8,128)(2,1)S(1)}, bf16[128,1792]{1,0:T(8,128)(2,1)S(1)}, u32[]{:S(2)}, u32[]{:S(2)}) collective-permute-start(bf16[128,1792]{1,0:T(8,128)(2,1)S(1)} %get-tuple-element.47), channel_id=1, source_target_pairs={{0,3},{1,0},{2,1},{3,2},{4,7},{5,4},{6,5},{7,6},{8,11},{9,8},{10,9... | collective-permute-start | bytes 1376264 | tf_op jit(solution)/shard_map/ppermute | solution.py:42
  92.4 5.4 %collective-permute-start.16 = (bf16[256,512]{1,0:T(8,128)(2,1)S(1)}, bf16[256,512]{1,0:T(8,128)(2,1)S(1)}, u32[]{:S(2)}, u32[]{:S(2)}) collective-permute-start(bf16[256,512]{1,0:T(8,128)(2,1)S(1)} %pad_maximum_fusion.6), channel_id=1, source_target_pairs={{0,64},{64,0},{1,65},{65,1},{2,66},{66,2},{3,67},{67,3},{4,68},{68... | collective-permute-start | bytes 786440 | tf_op jit(solution)/shard_map/ppermute | solution.py:37
  93.7 41.4 %collective-permute-start.21 = (bf16[128,1792]{1,0:T(8,128)(2,1)}, bf16[128,1792]{1,0:T(8,128)(2,1)}, u32[]{:S(2)}, u32[]{:S(2)}) collective-permute-start(bf16[128,1792]{1,0:T(8,128)(2,1)} %convolution_convert_fusion.2), channel_id=1, source_target_pairs={{0,4},{4,0},{1,5},{5,1},{2,6},{6,2},{3,7},{7,3},{8,12},{12,8},{9,1... | collective-permute-start | bytes 1376264 | tf_op jit(solution)/shard_map/ppermute | solution.py:37
  99.2 14.1 %collective-permute-start.17 = (bf16[128,1792]{1,0:T(8,128)(2,1)S(1)}, bf16[128,1792]{1,0:T(8,128)(2,1)S(1)}, u32[]{:S(2)}, u32[]{:S(2)}) collective-permute-start(bf16[128,1792]{1,0:T(8,128)(2,1)S(1)} %get-tuple-element.49), channel_id=1, source_target_pairs={{0,3},{1,0},{2,1},{3,2},{4,7},{5,4},{6,5},{7,6},{8,11},{9,8},{10,9... | collective-permute-start | bytes 1376264 | tf_op jit(solution)/shard_map/ppermute | solution.py:42
  100.5 17.2 %collective-permute-start.9 = (bf16[128,1792]{1,0:T(8,128)(2,1)S(1)}, bf16[128,1792]{1,0:T(8,128)(2,1)S(1)}, u32[]{:S(2)}, u32[]{:S(2)}) collective-permute-start(bf16[128,1792]{1,0:T(8,128)(2,1)S(1)} %fusion.11), channel_id=1, source_target_pairs={{0,1},{1,2},{2,3},{3,0},{4,5},{5,6},{6,7},{7,4},{8,9},{9,10},{10,1... | collective-permute-start | bytes 1376264 | tf_op jit(solution)/shard_map/ppermute | solution.py:42
  103.9 18.8 %collective-permute-start.19 = (bf16[128,1792]{1,0:T(8,128)(2,1)S(1)}, bf16[128,1792]{1,0:T(8,128)(2,1)S(1)}, u32[]{:S(2)}, u32[]{:S(2)}) collective-permute-start(bf16[128,1792]{1,0:T(8,128)(2,1)S(1)} %get-tuple-element.50), channel_id=1, source_target_pairs={{0,1},{1,2},{2,3},{3,0},{4,5},{5,6},{6,7},{7,4},{8,9},{9,10},{10,1... | collective-permute-start | bytes 1376264 | tf_op jit(solution)/shard_map/ppermute | solution.py:42
  113.3 31.2 %collective-permute-start.20 = (bf16[1792,256]{1,0:T(8,128)(2,1)}, bf16[1792,256]{1,0:T(8,128)(2,1)}, u32[]{:S(2)}, u32[]{:S(2)}) collective-permute-start(bf16[1792,256]{1,0:T(8,128)(2,1)} %convolution_convert_fusion), channel_id=1, source_target_pairs={{0,4},{4,0},{1,5},{5,1},{2,6},{6,2},{3,7},{7,3},{8,12},{12,8},{9,1... | collective-permute-start | bytes 2752520 | tf_op jit(solution)/shard_map/ppermute | solution.py:37
  117.7 12.1 %collective-permute-start.18 = (bf16[128,1792]{1,0:T(8,128)(2,1)S(1)}, bf16[128,1792]{1,0:T(8,128)(2,1)S(1)}, u32[]{:S(2)}, u32[]{:S(2)}) collective-permute-start(bf16[128,1792]{1,0:T(8,128)(2,1)S(1)} %fusion.8), channel_id=1, source_target_pairs={{0,3},{1,0},{2,1},{3,2},{4,7},{5,4},{6,5},{7,6},{8,11},{9,8},{10,9... | collective-permute-start | bytes 1376264 | tf_op jit(solution)/shard_map/ppermute | solution.py:42
  131.0 27.8 %all-to-all-start.1 = ((bf16[8,32,1792]{2,1,0:T(8,128)(2,1)}), bf16[8,32,1792]{2,1,0:T(8,128)(2,1)S(1)}, u32[]{:S(2)}, u32[]{:S(2)}) async-start(bf16[8,32,1792]{2,1,0:T(8,128)(2,1)} %pad_maximum_fusion.3), calls=%async_computation.1 | async-start | bytes 1835008 | tf_op jit(solution)/shard_map/all_to_all | solution.py:125
  146.4 1.4 copy-start.4
  146.4 1.7 %copy-start.5 = (bf16[2,1792,128]{2,1,0:T(8,128)(2,1)S(1)}, bf16[2,1792,128]{2,1,0:T(8,128)(2,1)}, u32[]{:S(2)}) copy-start(bf16[2,1792,128]{2,1,0:T(8,128)(2,1)} %param.15) | copy-start | bytes 2752516
  148.2 10.6 %copy-start.8 = (bf16[8,32,256]{2,1,0:T(8,128)(2,1)S(1)}, bf16[8,32,256]{2,1,0:T(8,128)(2,1)}, u32[]{:S(2)}) copy-start(bf16[8,32,256]{2,1,0:T(8,128)(2,1)} %get-tuple-element.24) | copy-start | bytes 393220
  (1 other events, 1.2 us)
